TPU v7x, 32 devices: a whole 2x2x4 slice. The times are simulated.
32 devices in a mesh: dp: 8 (over z, y), expert: 4 (over x, core).
Axes of the slice: x: 2, y: 2, z: 4, core: 2. Of those that a mesh axis runs over, the one named last changes fastest.
Arguments:
- tokens: bfloat16 [4096, 2048], P(('dp', 'expert')), may hold values from -6 to 6
- cotangent: bfloat16 [4096, 2048], P(('dp', 'expert')), may hold values from -6 to 6
- expert_ids: int32 [4096, 2], P(('dp', 'expert')), may hold values from 0 to 3, all different within a row; in each aligned block of 128 rows (0 to 127, 128 to 255, ...) at most 72 rows name the same one
- gate_values: bfloat16 [4096, 2], P(('dp', 'expert')), may hold values from 0.099609375 to 1
- gate_weights: bfloat16 [4, 2048, 512], P('expert'), may hold values from -0.125 to 0.125
- up_weights: bfloat16 [4, 2048, 512], P('expert'), may hold values from -0.125 to 0.125
- down_weights: bfloat16 [4, 512, 2048], P('expert'), may hold values from -0.25 to 0.25
Outputs:
- token_grads: bfloat16 [4096, 2048], P(('dp', 'expert'))
- down_grads: float32 [4, 512, 2048], P('expert', 'dp')
Inputs may be any that keep to these rules, and one draw needn't show every extreme that they name: `expert_ids`: within the rows of one device, each expert is named by at most 72 slots, and by exactly 72 slots in the rows of some device.
All inputs are finite; a program needn't handle non-finite values.
Results may differ from a plain program's by a relative error of at most 0.0065.
Values may be sent and summed in bfloat16 or wider, within the bound.
No kernel may reach another device: no remote copies, remote signals or barrier semaphores. Data moves between devices by JAX's collectives and lax.ppermute only.
A program may use at most 64 MiB of HBM per device.

v0:
```python
import functools

import jax
import jax.numpy as jnp
from jax import lax
from jax.experimental import pallas as pl
from jax.experimental.pallas import tpu as pltpu
from jax.sharding import PartitionSpec as P


F32 = jnp.float32
BF16 = jnp.bfloat16
LANES = 128
CHUNK_PARTS = (5, 4, 4, 3)
FIRST_BIT = (0, 1, 0, 0)
CONTRACT_COLS = (((1,), (1,)), ((), ()))
CONTRACT_ROWS = (((0,), (0,)), ((), ()))
VMEM_SPEC = pl.BlockSpec(memory_space=pltpu.VMEM)
HBM_SPEC = pl.BlockSpec(memory_space=pltpu.HBM)


def call(kernel, out_shapes, args, flops=0, vmem_mib=16, in_hbm=False, scratch=()):
    moved = sum(a.size * a.dtype.itemsize for a in args)
    moved += sum(jnp.dtype(o.dtype).itemsize * o.size for o in out_shapes)
    return pl.pallas_call(
        kernel,
        out_shape=out_shapes,
        in_specs=[HBM_SPEC if in_hbm else VMEM_SPEC] * len(args),
        out_specs=[VMEM_SPEC] * len(out_shapes),
        scratch_shapes=list(scratch),
        compiler_params=pltpu.CompilerParams(vmem_limit_bytes=vmem_mib * 1024 * 1024),
        cost_estimate=pl.CostEstimate(flops=flops, bytes_accessed=moved, transcendentals=0),
    )(*args)


def stacked(parts):
    return parts[0] if len(parts) == 1 else jnp.concatenate(parts, axis=0)


def gate_column(tagged, width):
    gates = stacked([t[:, width:] for t in tagged]).astype(F32)
    mine = lax.broadcasted_iota(jnp.int32, gates.shape, 1) == lax.axis_index("expert")
    return jnp.sum(jnp.where(mine, gates, 0.0), axis=1, keepdims=True)


def bit_of(axis, bit):
    return lax.rem(lax.div(lax.axis_index(axis), 1 << bit), 2)


def copy_all(sources, targets, sems):
    copies = [pltpu.make_async_copy(s, t, sems.at[i]) for i, (s, t) in enumerate(zip(sources, targets))]
    for c in copies:
        c.start()
    for c in copies:
        c.wait()


def load_kernel(count, *refs):
    copy_all(refs[:count], refs[count : 2 * count], refs[-1])


def prep_kernel(edges, choices, *refs):
    pieces = refs[3:-4]
    grads, ids, gates, sems = refs[-4:]
    copy_all(refs[:3], (grads, ids, gates), sems)
    experts = lax.broadcasted_iota(jnp.int32, (LANES, grads.shape[0]), 0)
    table = jnp.zeros(experts.shape, F32)
    values = gates[...].astype(F32)
    for k in range(choices):
        table = jnp.where(experts == ids[k : k + 1, :], values[k : k + 1, :], table)
    for at, piece in enumerate(pieces):
        low, high = edges[at], edges[at + 1]
        piece[:, : high - low] = grads[:, low:high]
    pieces[0][:, edges[1] :] = table.T.astype(BF16)


def hidden_kernel(count, *refs):
    rows = stacked([r[...] for r in refs[:count]])
    w_gate, w_up, hidden, gate_factor, up_factor = refs[count:]
    pre_gate = jnp.dot(rows, w_gate[...], preferred_element_type=F32)
    pre_up = jnp.dot(rows, w_up[...], preferred_element_type=F32)
    sig = jax.nn.sigmoid(pre_gate)
    act = pre_gate * sig
    hidden[...] = (act * pre_up).astype(BF16)
    gate_factor[...] = pre_up * sig * (1.0 + pre_gate * (1.0 - sig))
    up_factor[...] = act


def split_blocks(total, bit, mine, send, keep):
    blocks = send.shape[0] * 2
    size = total.shape[0] // blocks
    for side in range(2):

        @pl.when(mine == side)
        def _():
            for block in range(blocks):
                slot = (block >> (bit + 1) << bit) | (block & ((1 << bit) - 1))
                part = total[block * size : (block + 1) * size]
                if (block >> bit) & 1 == side:
                    keep[slot] = part
                else:
                    send[slot] = part.astype(BF16)


def down_kernel(count, width, bit, separate, *refs):
    hidden = stacked([r[...] for r in refs[:2]])
    tagged = refs[2 : 2 + count]
    parts = refs[2 + count : 2 + 2 * count] if separate else tagged
    send, keep = refs[-2:]
    wide = send.shape[2]
    gates = gate_column(tagged, width)
    grads = stacked([p[:, :wide] for p in parts])
    scaled = (gates * grads.astype(F32)).astype(BF16)
    total = lax.dot_general(hidden, scaled, CONTRACT_ROWS, preferred_element_type=F32)
    split_blocks(total, bit, bit_of("dp", bit), send, keep)


def merge_kernel(bit, place, keep_in, arrived, send, keep):
    blocks, size, wide = keep_in.shape
    total = keep_in[...] + arrived[...].astype(F32)
    split_blocks(total.reshape(blocks * size, wide), place, bit_of("dp", bit), send, keep)


def finish_kernel(edges, *refs):
    out = refs[-1]
    for at in range(len(edges) - 1):
        out[:, edges[at] : edges[at + 1]] = refs[2 * at][0] + refs[2 * at + 1][0].astype(F32)


def rows_kernel(count, edges, *refs):
    chunks = len(edges) - 1
    gates = gate_column(refs[:count], edges[1])
    gate_factor, up_factor, w_gate, w_up, w_down = refs[chunks * count : chunks * count + 5]
    outs = refs[chunks * count + 5 :]
    back = None
    for c in range(chunks):
        low, high = edges[c], edges[c + 1]
        part = stacked([r[:, : high - low] for r in refs[c * count : (c + 1) * count]])
        scaled = (gates * part.astype(F32)).astype(BF16)
        term = lax.dot_general(scaled, w_down[:, low:high], CONTRACT_COLS, preferred_element_type=F32)
        back = term if back is None else back + term
    gate_back = (back * gate_factor[...]).astype(BF16)
    up_back = (back * up_factor[...]).astype(BF16)
    total = lax.dot_general(gate_back, w_gate[...], CONTRACT_COLS, preferred_element_type=F32)
    total += lax.dot_general(up_back, w_up[...], CONTRACT_COLS, preferred_element_type=F32)
    total = total.astype(BF16)
    size = total.shape[0] // count
    for i, out in enumerate(outs):
        out[...] = total[i * size : (i + 1) * size]


def sum_kernel(*refs):
    total = refs[0][...].astype(F32)
    for r in refs[1:-1]:
        total = total + r[...].astype(F32)
    refs[-1][...] = total.astype(BF16)


def swap(value, axis, bit):
    size = lax.axis_size(axis)
    return lax.ppermute(value, axis, [(i, i ^ (1 << bit)) for i in range(size)])


def spread(value, bits):
    out = [value]
    for bit in bits:
        out += [swap(v, "expert", bit) for v in out]
    return out


def column_edges(width):
    parts = sum(CHUNK_PARTS)
    if width % (LANES * parts):
        return (0, width)
    edges = [0]
    for p in CHUNK_PARTS:
        edges.append(edges[-1] + p * (width // parts))
    return tuple(edges)


def narrow_body(tokens, cotangent, expert_ids, gate_values, gate_weights, up_weights, down_weights):
    experts, dp = lax.axis_size("expert"), lax.axis_size("dp")
    rows, width = tokens.shape
    hidden_width = gate_weights.shape[2]
    choices = expert_ids.shape[1]
    dp_bits = dp.bit_length() - 1
    top = experts.bit_length() - 2
    low = list(range(top))
    edges = column_edges(width)
    chunks = len(edges) - 1
    widths = [b - a for a, b in zip(edges, edges[1:])]
    struct = jax.ShapeDtypeStruct

    far_first = swap(tokens, "expert", top)
    near_tokens = spread(tokens, low)
    pieces = call(
        functools.partial(prep_kernel, edges, choices),
        [struct((rows, w + (LANES if c == 0 else 0)), BF16) for c, w in enumerate(widths)],
        [cotangent, expert_ids.T, gate_values.T],
        vmem_mib=56,
        in_hbm=True,
        scratch=[
            pltpu.VMEM((rows, width), BF16),
            pltpu.VMEM((choices, rows), jnp.int32),
            pltpu.VMEM((choices, rows), BF16),
            pltpu.SemaphoreType.DMA((3,)),
        ],
    )
    kept = [gate_weights[0], up_weights[0], down_weights[0], tokens]
    w_gate, w_up, w_down, own_tokens = call(
        functools.partial(load_kernel, len(kept)),
        [struct(a.shape, a.dtype) for a in kept],
        kept,
        vmem_mib=46,
        in_hbm=True,
        scratch=[pltpu.SemaphoreType.DMA((len(kept),))],
    )
    far_pieces = [swap(p, "expert", top) for p in pieces]
    near_pieces = [spread(p, low) for p in pieces]
    far_tokens = spread(far_first, low)
    far_pieces = [spread(p, low) for p in far_pieces]
    count = len(near_tokens)
    group_rows = count * rows
    mat = 2 * group_rows * width * hidden_width

    def hidden_of(blocks):
        shape = (group_rows, hidden_width)
        return call(
            functools.partial(hidden_kernel, count),
            [struct(shape, t) for t in (BF16, F32, F32)],
            [*blocks, w_gate, w_up],
            2 * mat,
        )

    def rows_of(groups, factors):
        args = [p for group in groups for p in group] + [*factors, w_gate, w_up, w_down]
        return call(
            functools.partial(rows_kernel, count, edges),
            [struct((rows, width), BF16)] * count,
            args,
            3 * mat,
        )

    def gathered(blocks):
        for bit in reversed(low):
            half = len(blocks) // 2
            got = [swap(b, "expert", bit) for b in blocks[half:]]
            if half == 1:
                return [blocks[0], got[0]]
            blocks = [
                call(sum_kernel, [struct((rows, width), BF16)], [a, g])[0]
                for a, g in zip(blocks, got)
            ]
        return blocks

    near_hidden, *near_factors = hidden_of([own_tokens, *near_tokens[1:]])
    near_rows = rows_of(near_pieces, near_factors)
    near_terms = gathered(near_rows)
    far_hidden, *far_factors = hidden_of(far_tokens)

    block = hidden_width // dp
    down_terms = []
    for c in range(chunks):
        order = list(range(dp_bits))
        first = FIRST_BIT[c] if dp_bits > 1 else 0
        order[0], order[first] = order[first], order[0]
        tagged = near_pieces[0] + far_pieces[0]
        parts = near_pieces[c] + far_pieces[c] if c else []
        send, keep = call(
            functools.partial(down_kernel, len(tagged), widths[0], order[0], c > 0),
            [struct((dp // 2, block, widths[c]), t) for t in (BF16, F32)],
            [near_hidden, far_hidden, *tagged, *parts],
            2 * mat * widths[c] // width,
        )
        left = list(range(dp_bits))
        for at, bit in enumerate(order):
            arrived = swap(send, "dp", bit)
            left.remove(bit)
            if at + 1 < dp_bits:
                nxt = order[at + 1]
                half = struct((keep.shape[0] // 2, block, widths[c]), F32)
                send, keep = call(
                    functools.partial(merge_kernel, nxt, left.index(nxt)),
                    [struct(half.shape, BF16), half],
                    [keep, arrived],
                )
        down_terms += [keep, arrived]
    down = call(
        functools.partial(finish_kernel, edges), [struct((block, width), F32)], down_terms
    )[0]

    far_rows = rows_of(far_pieces, far_factors)
    far_terms = gathered(far_rows)
    if len(far_terms) > 1:
        far_terms = call(sum_kernel, [struct((rows, width), BF16)], far_terms)
    far_total = swap(far_terms[0], "expert", top)
    token_grads = call(sum_kernel, [struct((rows, width), BF16)], [*near_terms, far_total])[0]
    return (token_grads, down[None])


def body(*args):
    return narrow_body(*args)


def wide_body(tokens, cotangent, expert_ids, gate_values, gate_weights, up_weights, down_weights):
    experts_here = lax.axis_size("expert")
    tok_count, model_width = tokens.shape
    choices_per = expert_ids.shape[1]
    capacity = tok_count * choices_per * 9 // (8 * experts_here)
    slot_total = tok_count * choices_per
    flat_ids = expert_ids.reshape(slot_total)
    columns = jnp.arange(experts_here, dtype=jnp.int32)
    one_hot = (flat_ids[:, None] == columns[None, :]).astype(jnp.int32)
    earlier = jnp.cumsum(one_hot, axis=0) - one_hot
    position = jnp.sum(one_hot * earlier, axis=1)
    target = flat_ids * capacity + position
    slot_ids = jnp.arange(slot_total, dtype=jnp.int32)
    source = jnp.full((experts_here * capacity,), slot_total, jnp.int32).at[target].set(slot_ids)
    source_token = source // choices_per
    sent_rows = jnp.take(tokens, source_token, axis=0, mode="fill", fill_value=0).reshape(
        experts_here, capacity, model_width
    )
    sent_grads = jnp.take(cotangent, source_token, axis=0, mode="fill", fill_value=0).reshape(
        experts_here, capacity, model_width
    )
    sent_gates = jnp.take(
        gate_values.reshape(slot_total), source, axis=0, mode="fill", fill_value=0
    ).reshape(experts_here, capacity)
    w_gate = gate_weights[0]
    w_up = up_weights[0]
    w_down = down_weights[0]
    arrived = lax.all_to_all(sent_rows, "expert", split_axis=0, concat_axis=0, tiled=True).reshape(
        -1, model_width
    )
    pre_gate = jnp.dot(arrived, w_gate, preferred_element_type=jnp.float32)
    pre_up = jnp.dot(arrived, w_up, preferred_element_type=jnp.float32)
    sigmoid_of = jax.nn.sigmoid(pre_gate)
    activated = pre_gate * sigmoid_of
    hidden = (activated * pre_up).astype(jnp.bfloat16)
    arrived_grads, arrived_gates = (
        lax.all_to_all(sent_grads, "expert", split_axis=0, concat_axis=0, tiled=True),
        lax.all_to_all(sent_gates, "expert", split_axis=0, concat_axis=0, tiled=True),
    )
    scaled = (
        arrived_gates.reshape(-1)[:, None].astype(jnp.float32)
        * arrived_grads.reshape(-1, model_width).astype(jnp.float32)
    ).astype(jnp.bfloat16)
    hidden_back = lax.dot_general(scaled, w_down, CONTRACT_COLS, preferred_element_type=jnp.float32)
    gate_back = (hidden_back * pre_up * sigmoid_of * (1.0 + pre_gate * (1.0 - sigmoid_of))).astype(
        jnp.bfloat16
    )
    up_back = (hidden_back * activated).astype(jnp.bfloat16)
    row_grads = lax.dot_general(gate_back, w_gate, CONTRACT_COLS, preferred_element_type=jnp.float32)
    row_grads = (
        row_grads
        + lax.dot_general(up_back, w_up, CONTRACT_COLS, preferred_element_type=jnp.float32)
    ).astype(jnp.bfloat16)
    returned = lax.all_to_all(
        row_grads.reshape(experts_here, capacity, model_width),
        "expert",
        split_axis=0,
        concat_axis=0,
        tiled=True,
    )
    picked = jnp.take(returned.reshape(-1, model_width), target, axis=0).astype(jnp.float32)
    token_grads = jnp.sum(picked.reshape(tok_count, choices_per, model_width), axis=1).astype(
        jnp.bfloat16
    )
    down_part = lax.psum_scatter(
        lax.dot_general(
            hidden, scaled, (((0,), (0,)), ((), ())), preferred_element_type=jnp.float32
        ),
        "dp",
        scatter_dimension=0,
        tiled=True,
    )
    return (token_grads, down_part[None])


def power_of_two(n):
    return n > 1 and n & (n - 1) == 0


def solution(mesh):
    experts, dp = mesh.shape["expert"], mesh.shape["dp"]
    narrow = power_of_two(experts) and power_of_two(dp) and experts <= 4
    return jax.shard_map(
        body if narrow else wide_body,
        mesh=mesh,
        in_specs=(
            P(("dp", "expert"), None),
            P(("dp", "expert"), None),
            P(("dp", "expert"), None),
            P(("dp", "expert"), None),
            P("expert", None, None),
            P("expert", None, None),
            P("expert", None, None),
        ),
        out_specs=(P(("dp", "expert"), None), P("expert", "dp", None)),
        check_vma=False,
    )
```

profile of v0, /device:TPU:0, one launch (start us, length us, event | category | flops | bytes accessed | tf_op | source)
XLA Modules:
  0.0 84.0 jit_solution(13679391164980069700)
XLA Ops:
  0.6 3.0 %collective-permute-start.14 = (bf16[128,2048]{1,0:T(8,128)(2,1)}, bf16[128,2048]{1,0:T(8,128)(2,1)S(1)}, u32[]{:S(2)}, u32[]{:S(2)}) collective-permute-start(bf16[128,2048]{1,0:T(8,128)(2,1)} %refs_3_.1), channel_id=1, source_target_pairs={{0,2},{1,3},{2,0},{3,1},{4,6},{5,7},{6,4},{7,5},{8,10},{9,11},{10,... | collective-permute-start | bytes 1572872 | tf_op jit(solution)/shard_map/ppermute | solution.py:161
  3.7 12.1 %collective-permute-done.14.refs_0_ = bf16[128,2048]{1,0:T(8,128)(2,1)S(1)} collective-permute-done((bf16[128,2048]{1,0:T(8,128)(2,1)}, bf16[128,2048]{1,0:T(8,128)(2,1)S(1)}, u32[]{:S(2)}, u32[]{:S(2)}) %collective-permute-start.14) | collective-permute-done | bytes 524320 | tf_op jit(solution)/shard_map/ppermute | solution.py:161
  15.8 1.9 %shard_map.86 = (bf16[128,768]{1,0:T(8,128)(2,1)}, bf16[128,512]{1,0:T(8,128)(2,1)}, bf16[128,512]{1,0:T(8,128)(2,1)}, bf16[128,384]{1,0:T(8,128)(2,1)}) custom-call(bf16[128,2048]{1,0:T(8,128)(2,1)} %refs_0_.1, s32[2,128]{1,0:T(2,128)} %bitcast.10, bf16[2,128]{1,0:T(2,128)(2,1)} %bitcast.11), custom_call_target="tpu_custom_call" | custom-call | bytes 1082880 | tf_op jit(solution)/shard_map/pallas_call | solution.py:25
  17.7 1.8 %collective-permute-start.6 = (bf16[128,768]{1,0:T(8,128)(2,1)}, bf16[128,768]{1,0:T(8,128)(2,1)S(1)}, u32[]{:S(2)}, u32[]{:S(2)}) collective-permute-start(bf16[128,768]{1,0:T(8,128)(2,1)} %get-tuple-element.44.refs_0_.refs_2_), channel_id=1, source_target_pairs={{0,2},{1,3},{2,0},{3,1},{4,6},{5,7},{6,4},{7,5},{8,10},{9,11},{10,... | collective-permute-start | bytes 589832 | tf_op jit(solution)/shard_map/ppermute | solution.py:161
  19.5 0.3 collective-permute-start.12
  19.8 1.7 %collective-permute-start.8 = (bf16[128,512]{1,0:T(8,128)(2,1)}, bf16[128,512]{1,0:T(8,128)(2,1)S(1)}, u32[]{:S(2)}, u32[]{:S(2)}) collective-permute-start(bf16[128,512]{1,0:T(8,128)(2,1)} %get-tuple-element.45.refs_2_.refs_6_), channel_id=1, source_target_pairs={{0,2},{1,3},{2,0},{3,1},{4,6},{5,7},{6,4},{7,5},{8,10},{9,11},{10,... | collective-permute-start | bytes 393224 | tf_op jit(solution)/shard_map/ppermute | solution.py:161
  21.5 0.3 collective-permute-start.10
  21.8 3.9 %collective-permute-done.6.refs_0_.refs_4_ = bf16[128,768]{1,0:T(8,128)(2,1)S(1)} collective-permute-done((bf16[128,768]{1,0:T(8,128)(2,1)}, bf16[128,768]{1,0:T(8,128)(2,1)S(1)}, u32[]{:S(2)}, u32[]{:S(2)}) %collective-permute-start.6) | collective-permute-done | bytes 196640 | tf_op jit(solution)/shard_map/ppermute | solution.py:161
  25.7 0.0 collective-permute-start.7
  25.7 2.1 %collective-permute-done.12.refs_6_.refs_8_ = bf16[128,384]{1,0:T(8,128)(2,1)S(1)} collective-permute-done((bf16[128,384]{1,0:T(8,128)(2,1)}, bf16[128,384]{1,0:T(8,128)(2,1)S(1)}, u32[]{:S(2)}, u32[]{:S(2)}) %collective-permute-start.12) | collective-permute-done | bytes 98336 | tf_op jit(solution)/shard_map/ppermute | solution.py:161
  27.9 0.0 collective-permute-start.4
  27.9 2.8 %collective-permute-done.8.refs_2_.refs_8_ = bf16[128,512]{1,0:T(8,128)(2,1)S(1)} collective-permute-done((bf16[128,512]{1,0:T(8,128)(2,1)}, bf16[128,512]{1,0:T(8,128)(2,1)S(1)}, u32[]{:S(2)}, u32[]{:S(2)}) %collective-permute-start.8) | collective-permute-done | bytes 131104 | tf_op jit(solution)/shard_map/ppermute | solution.py:161
  30.7 2.3 %collective-permute-done.10.refs_4_.refs_8_ = bf16[128,512]{1,0:T(8,128)(2,1)S(1)} collective-permute-done((bf16[128,512]{1,0:T(8,128)(2,1)}, bf16[128,512]{1,0:T(8,128)(2,1)S(1)}, u32[]{:S(2)}, u32[]{:S(2)}) %collective-permute-start.10) | collective-permute-done | bytes 131104 | tf_op jit(solution)/shard_map/ppermute | solution.py:161
  33.0 0.0 collective-permute-start.11
  33.0 1.0 %copy-done.3 = bf16[128,2048]{1,0:T(8,128)(2,1)S(1)} copy-done((bf16[128,2048]{1,0:T(8,128)(2,1)S(1)}, bf16[128,2048]{1,0:T(8,128)(2,1)}, u32[]{:S(2)}) %copy-start.3) | copy-done | bytes 524312
  34.1 2.9 %shard_map.87 = (bf16[2048,512]{1,0:T(8,128)(2,1)S(1)}, bf16[2048,512]{1,0:T(8,128)(2,1)S(1)}, bf16[512,2048]{1,0:T(8,128)(2,1)S(1)}, bf16[128,2048]{1,0:T(8,128)(2,1)S(1)}) custom-call(bf16[2048,512]{1,0:T(8,128)(2,1)} %bitcast.6, bf16[2048,512]{1,0:T(8,128)(2,1)} %bitcast.7, bf16[512,2048]{1,0:T(8,128)(2,1)} %bitcast.8, bf16[128,2048]{1,0:T(8,128)(2,1)S(1)} %copy-done.3), custom_call_target="tpu_custom_call" | custom-call | bytes 13631488 | tf_op jit(solution)/shard_map/pallas_call | solution.py:25
  37.0 0.0 collective-permute-done.15.refs_1_
  37.0 0.6 collective-permute-start.13
  37.5 1.3 %shard_map.90 = (bf16[256,512]{1,0:T(8,128)(2,1)S(1)}, f32[256,512]{1,0:T(8,128)S(1)}, f32[256,512]{1,0:T(8,128)S(1)}) custom-call(bf16[128,2048]{1,0:T(8,128)(2,1)S(1)} %collective-permute-done.14.refs_0_, bf16[128,2048]{1,0:T(8,128)(2,1)S(1)} %collective-permute-done.15.refs_1_, bf16[2048,512]{1,0:T(8,128)(2,1)S(1)} %get-tuple-element.49.refs_2_.refs_10_, ...), custom_call_target="tpu_custom_call" | custom-call | flops 1073741824 | bytes 6553600 | tf_op jit(solution)/shard_map/pallas_call | solution.py:25
  38.9 0.0 collective-permute-done.11.refs_5_.refs_9_
  38.9 0.0 collective-permute-done.7.refs_1_.refs_5_
  38.9 0.0 copy-start
  38.9 0.0 copy-start.2
  38.9 2.0 %shard_map.91 = (bf16[128,2048]{1,0:T(8,128)(2,1)S(1)}, bf16[128,2048]{1,0:T(8,128)(2,1)S(1)}) custom-call(bf16[128,768]{1,0:T(8,128)(2,1)S(1)} %collective-permute-done.6.refs_0_.refs_4_, bf16[128,768]{1,0:T(8,128)(2,1)S(1)} %collective-permute-done.7.refs_1_.refs_5_, bf16[128,512]{1,0:T(8,128)(2,1)S(1)} %collective-permute-done.8.refs_2_.refs_8_, ...), custom_call_target="tpu_custom_call" | custom-call | flops 1610612736 | bytes 9502720 | tf_op jit(solution)/shard_map/pallas_call | solution.py:25
  40.9 0.1 collective-permute-start.16
  41.0 0.5 collective-permute-start
  41.5 0.1 collective-permute-start.1
  41.6 0.4 collective-permute-start.3
  42.0 0.0 collective-permute-done.4.refs_1_
  42.0 0.1 collective-permute-start.2
  42.1 1.3 %shard_map.88 = (bf16[256,512]{1,0:T(8,128)(2,1)S(1)}, f32[256,512]{1,0:T(8,128)S(1)}, f32[256,512]{1,0:T(8,128)S(1)}) custom-call(bf16[128,2048]{1,0:T(8,128)(2,1)S(1)} %get-tuple-element.48.refs_0_, bf16[128,2048]{1,0:T(8,128)(2,1)S(1)} %collective-permute-done.4.refs_1_, bf16[2048,512]{1,0:T(8,128)(2,1)S(1)} %get-tuple-element.49.refs_2_.refs_10_, ...), custom_call_target="tpu_custom_call" | custom-call | flops 1073741824 | bytes 6553600 | tf_op jit(solution)/shard_map/pallas_call | solution.py:25
  43.4 0.1 collective-permute-done.3.refs_7_
  43.5 0.0 collective-permute-done.refs_1_.refs_3_
  43.5 0.6 shard_map.103
  44.1 1.8 %collective-permute-start.27 = (bf16[4,64,384]{2,1,0:T(8,128)(2,1)S(1)}, bf16[4,64,384]{2,1,0:T(8,128)(2,1)S(1)}, u32[]{:S(2)}, u32[]{:S(2)}) collective-permute-start(bf16[4,64,384]{2,1,0:T(8,128)(2,1)S(1)} %get-tuple-element.81), channel_id=1, source_target_pairs={{0,4},{4,0},{8,12},{12,8},{16,20},{20,16},{24,28},{28,24},{1,5},{5... | collective-permute-start | bytes 589832 | tf_op jit(solution)/shard_map/ppermute | solution.py:161
  45.9 0.6 shard_map.97
  46.5 1.7 %collective-permute-start.21 = (bf16[4,64,512]{2,1,0:T(8,128)(2,1)S(1)}, bf16[4,64,512]{2,1,0:T(8,128)(2,1)S(1)}, u32[]{:S(2)}, u32[]{:S(2)}) collective-permute-start(bf16[4,64,512]{2,1,0:T(8,128)(2,1)S(1)} %get-tuple-element.69), channel_id=1, source_target_pairs={{0,8},{4,12},{8,0},{12,4},{16,24},{20,28},{24,16},{28,20},{1,9},{5... | collective-permute-start | bytes 786440 | tf_op jit(solution)/shard_map/ppermute | solution.py:161
  48.2 0.8 shard_map.94
  48.9 0.6 collective-permute-start.18
  49.5 2.0 %shard_map.89 = (bf16[128,2048]{1,0:T(8,128)(2,1)S(1)}, bf16[128,2048]{1,0:T(8,128)(2,1)S(1)}) custom-call(bf16[128,768]{1,0:T(8,128)(2,1)S(1)} %copy-done, bf16[128,768]{1,0:T(8,128)(2,1)S(1)} %collective-permute-done.refs_1_.refs_3_, bf16[128,512]{1,0:T(8,128)(2,1)S(1)} %copy-done.2, bf16[128,512]{1,0:T(8,128)(2,1)S(1)} %collective-permute-done.1.refs_3_.refs_7_, ...), custom_call_target="tpu_custom_call" | custom-call | flops 1610612736 | bytes 9502720 | tf_op jit(solution)/shard_map/pallas_call | solution.py:25
  51.5 0.1 collective-permute-start.5
  51.6 0.0 collective-permute-done.16.refs_1_
  51.6 0.1 shard_map.92
  51.7 1.6 %collective-permute-start.17 = (bf16[128,2048]{1,0:T(8,128)(2,1)S(1)}, bf16[128,2048]{1,0:T(8,128)(2,1)S(1)}, u32[]{:S(2)}, u32[]{:S(2)}) collective-permute-start(bf16[128,2048]{1,0:T(8,128)(2,1)S(1)} %shard_map.92), channel_id=1, source_target_pairs={{0,2},{1,3},{2,0},{3,1},{4,6},{5,7},{6,4},{7,5},{8,10},{9,11},{10,... | collective-permute-start | bytes 1572872 | tf_op jit(solution)/shard_map/ppermute | solution.py:161
  53.3 0.6 shard_map.100
  53.9 1.6 %collective-permute-start.24 = (bf16[4,64,512]{2,1,0:T(8,128)(2,1)S(1)}, bf16[4,64,512]{2,1,0:T(8,128)(2,1)S(1)}, u32[]{:S(2)}, u32[]{:S(2)}) collective-permute-start(bf16[4,64,512]{2,1,0:T(8,128)(2,1)S(1)} %get-tuple-element.75), channel_id=1, source_target_pairs={{0,4},{4,0},{8,12},{12,8},{16,20},{20,16},{24,28},{28,24},{1,5},{5... | collective-permute-start | bytes 786440 | tf_op jit(solution)/shard_map/ppermute | solution.py:161
  55.5 0.1 shard_map.104
  55.6 4.0 %collective-permute-done.18.arrived = bf16[4,64,640]{2,1,0:T(8,128)(2,1)S(1)} collective-permute-done((bf16[4,64,640]{2,1,0:T(8,128)(2,1)S(1)}, bf16[4,64,640]{2,1,0:T(8,128)(2,1)S(1)}, u32[]{:S(2)}, u32[]{:S(2)}) %collective-permute-start.18) | collective-permute-done | bytes 327712 | tf_op jit(solution)/shard_map/ppermute | solution.py:161
  59.6 1.2 %collective-permute-start.28 = (bf16[2,64,384]{2,1,0:T(8,128)(2,1)S(1)}, bf16[2,64,384]{2,1,0:T(8,128)(2,1)S(1)}, u32[]{:S(2)}, u32[]{:S(2)}) collective-permute-start(bf16[2,64,384]{2,1,0:T(8,128)(2,1)S(1)} %get-tuple-element.83), channel_id=1, source_target_pairs={{0,8},{4,12},{8,0},{12,4},{16,24},{20,28},{24,16},{28,20},{1,9},{5... | collective-permute-start | bytes 294920 | tf_op jit(solution)/shard_map/ppermute | solution.py:161
  60.7 0.1 shard_map.95
  60.9 0.9 %collective-permute-start.19 = (bf16[2,64,640]{2,1,0:T(8,128)(2,1)S(1)}, bf16[2,64,640]{2,1,0:T(8,128)(2,1)S(1)}, u32[]{:S(2)}, u32[]{:S(2)}) collective-permute-start(bf16[2,64,640]{2,1,0:T(8,128)(2,1)S(1)} %get-tuple-element.65), channel_id=1, source_target_pairs={{0,8},{4,12},{8,0},{12,4},{16,24},{20,28},{24,16},{28,20},{1,9},{5... | collective-permute-start | bytes 491528 | tf_op jit(solution)/shard_map/ppermute | solution.py:161
  61.8 0.1 shard_map.98
  61.9 2.1 %collective-permute-done.24.arrived = bf16[4,64,512]{2,1,0:T(8,128)(2,1)S(1)} collective-permute-done((bf16[4,64,512]{2,1,0:T(8,128)(2,1)S(1)}, bf16[4,64,512]{2,1,0:T(8,128)(2,1)S(1)}, u32[]{:S(2)}, u32[]{:S(2)}) %collective-permute-start.24) | collective-permute-done | bytes 262176 | tf_op jit(solution)/shard_map/ppermute | solution.py:161
  64.0 1.7 %collective-permute-start.22 = (bf16[2,64,512]{2,1,0:T(8,128)(2,1)S(1)}, bf16[2,64,512]{2,1,0:T(8,128)(2,1)S(1)}, u32[]{:S(2)}, u32[]{:S(2)}) collective-permute-start(bf16[2,64,512]{2,1,0:T(8,128)(2,1)S(1)} %get-tuple-element.71), channel_id=1, source_target_pairs={{0,4},{4,0},{8,12},{12,8},{16,20},{20,16},{24,28},{28,24},{1,5},{5... | collective-permute-start | bytes 393224 | tf_op jit(solution)/shard_map/ppermute | solution.py:161
  65.7 0.1 shard_map.101
  65.8 1.6 %collective-permute-start.25 = (bf16[2,64,512]{2,1,0:T(8,128)(2,1)S(1)}, bf16[2,64,512]{2,1,0:T(8,128)(2,1)S(1)}, u32[]{:S(2)}, u32[]{:S(2)}) collective-permute-start(bf16[2,64,512]{2,1,0:T(8,128)(2,1)S(1)} %get-tuple-element.77), channel_id=1, source_target_pairs={{0,8},{4,12},{8,0},{12,4},{16,24},{20,28},{24,16},{28,20},{1,9},{5... | collective-permute-start | bytes 393224 | tf_op jit(solution)/shard_map/ppermute | solution.py:161
  67.5 2.7 %collective-permute-start.29 = (bf16[1,64,384]{2,1,0:T(8,128)(2,1)S(1)}, bf16[1,64,384]{2,1,0:T(8,128)(2,1)S(1)}, u32[]{:S(2)}, u32[]{:S(2)}) collective-permute-start(bf16[1,64,384]{2,1,0:T(8,128)(2,1)S(1)} %get-tuple-element.85), channel_id=1, source_target_pairs={{0,16},{4,20},{8,24},{12,28},{16,0},{20,4},{24,8},{28,12},{1,17},{... | collective-permute-start | bytes 147464 | tf_op jit(solution)/shard_map/ppermute | solution.py:161
  70.2 1.5 %collective-permute-start.20 = (bf16[1,64,640]{2,1,0:T(8,128)(2,1)S(1)}, bf16[1,64,640]{2,1,0:T(8,128)(2,1)S(1)}, u32[]{:S(2)}, u32[]{:S(2)}) collective-permute-start(bf16[1,64,640]{2,1,0:T(8,128)(2,1)S(1)} %get-tuple-element.67), channel_id=1, source_target_pairs={{0,16},{4,20},{8,24},{12,28},{16,0},{20,4},{24,8},{28,12},{1,17},{... | collective-permute-start | bytes 245768 | tf_op jit(solution)/shard_map/ppermute | solution.py:161
  71.8 2.5 %collective-permute-start.23 = (bf16[1,64,512]{2,1,0:T(8,128)(2,1)S(1)}, bf16[1,64,512]{2,1,0:T(8,128)(2,1)S(1)}, u32[]{:S(2)}, u32[]{:S(2)}) collective-permute-start(bf16[1,64,512]{2,1,0:T(8,128)(2,1)S(1)} %get-tuple-element.73), channel_id=1, source_target_pairs={{0,16},{4,20},{8,24},{12,28},{16,0},{20,4},{24,8},{28,12},{1,17},{... | collective-permute-start | bytes 196616 | tf_op jit(solution)/shard_map/ppermute | solution.py:161
  74.4 1.0 %collective-permute-start.26 = (bf16[1,64,512]{2,1,0:T(8,128)(2,1)S(1)}, bf16[1,64,512]{2,1,0:T(8,128)(2,1)S(1)}, u32[]{:S(2)}, u32[]{:S(2)}) collective-permute-start(bf16[1,64,512]{2,1,0:T(8,128)(2,1)S(1)} %get-tuple-element.79), channel_id=1, source_target_pairs={{0,16},{4,20},{8,24},{12,28},{16,0},{20,4},{24,8},{28,12},{1,17},{... | collective-permute-start | bytes 196616 | tf_op jit(solution)/shard_map/ppermute | solution.py:161
  75.4 5.3 %collective-permute-done.23.refs_3_ = bf16[1,64,512]{2,1,0:T(8,128)(2,1)S(1)} collective-permute-done((bf16[1,64,512]{2,1,0:T(8,128)(2,1)S(1)}, bf16[1,64,512]{2,1,0:T(8,128)(2,1)S(1)}, u32[]{:S(2)}, u32[]{:S(2)}) %collective-permute-start.23) | collective-permute-done | bytes 65568 | tf_op jit(solution)/shard_map/ppermute | solution.py:161
  80.7 1.5 %collective-permute-done.26.refs_5_ = bf16[1,64,512]{2,1,0:T(8,128)(2,1)S(1)} collective-permute-done((bf16[1,64,512]{2,1,0:T(8,128)(2,1)S(1)}, bf16[1,64,512]{2,1,0:T(8,128)(2,1)S(1)}, u32[]{:S(2)}, u32[]{:S(2)}) %collective-permute-start.26) | collective-permute-done | bytes 65568 | tf_op jit(solution)/shard_map/ppermute | solution.py:161
  82.2 0.8 shard_map.106
  83.0 1.0 %shard_map.93 = bf16[128,2048]{1,0:T(8,128)(2,1)} custom-call(bf16[128,2048]{1,0:T(8,128)(2,1)S(1)} %get-tuple-element.54.refs_0_, bf16[128,2048]{1,0:T(8,128)(2,1)S(1)} %collective-permute-done.5.refs_1_, bf16[128,2048]{1,0:T(8,128)(2,1)S(1)} %collective-permute-done.17.refs_2_), custom_call_target="tpu_custom_call" | custom-call | bytes 2097152 | tf_op jit(solution)/shard_map/pallas_call | solution.py:25
  (27 shorter events, 0.2 us)
Async XLA Ops:
  0.6 15.2 %collective-permute-start.14 = (bf16[128,2048]{1,0:T(8,128)(2,1)}, bf16[128,2048]{1,0:T(8,128)(2,1)S(1)}, u32[]{:S(2)}, u32[]{:S(2)}) collective-permute-start(bf16[128,2048]{1,0:T(8,128)(2,1)} %refs_3_.1), channel_id=1, source_target_pairs={{0,2},{1,3},{2,0},{3,1},{4,6},{5,7},{6,4},{7,5},{8,10},{9,11},{10,... | collective-permute-start | bytes 1572872 | tf_op jit(solution)/shard_map/ppermute | solution.py:161
  15.8 21.2 %collective-permute-start.15 = (bf16[128,2048]{1,0:T(8,128)(2,1)S(1)}, bf16[128,2048]{1,0:T(8,128)(2,1)S(1)}, u32[]{:S(2)}, u32[]{:S(2)}) collective-permute-start(bf16[128,2048]{1,0:T(8,128)(2,1)S(1)} %collective-permute-done.14.refs_0_), channel_id=1, source_target_pairs={{0,1},{1,0},{2,3},{3,2},{4,5},{5,4},{6,7},{7,6},{8,9},{9,8},{10,11... | collective-permute-start | bytes 1572872 | tf_op jit(solution)/shard_map/ppermute | solution.py:161
  17.7 8.0 %collective-permute-start.6 = (bf16[128,768]{1,0:T(8,128)(2,1)}, bf16[128,768]{1,0:T(8,128)(2,1)S(1)}, u32[]{:S(2)}, u32[]{:S(2)}) collective-permute-start(bf16[128,768]{1,0:T(8,128)(2,1)} %get-tuple-element.44.refs_0_.refs_2_), channel_id=1, source_target_pairs={{0,2},{1,3},{2,0},{3,1},{4,6},{5,7},{6,4},{7,5},{8,10},{9,11},{10,... | collective-permute-start | bytes 589832 | tf_op jit(solution)/shard_map/ppermute | solution.py:161
  19.5 8.4 %collective-permute-start.12 = (bf16[128,384]{1,0:T(8,128)(2,1)}, bf16[128,384]{1,0:T(8,128)(2,1)S(1)}, u32[]{:S(2)}, u32[]{:S(2)}) collective-permute-start(bf16[128,384]{1,0:T(8,128)(2,1)} %get-tuple-element.47.refs_6_), channel_id=1, source_target_pairs={{0,2},{1,3},{2,0},{3,1},{4,6},{5,7},{6,4},{7,5},{8,10},{9,11},{10,... | collective-permute-start | bytes 294920 | tf_op jit(solution)/shard_map/ppermute | solution.py:161
  19.8 10.9 %collective-permute-start.8 = (bf16[128,512]{1,0:T(8,128)(2,1)}, bf16[128,512]{1,0:T(8,128)(2,1)S(1)}, u32[]{:S(2)}, u32[]{:S(2)}) collective-permute-start(bf16[128,512]{1,0:T(8,128)(2,1)} %get-tuple-element.45.refs_2_.refs_6_), channel_id=1, source_target_pairs={{0,2},{1,3},{2,0},{3,1},{4,6},{5,7},{6,4},{7,5},{8,10},{9,11},{10,... | collective-permute-start | bytes 393224 | tf_op jit(solution)/shard_map/ppermute | solution.py:161
  21.5 11.5 %collective-permute-start.10 = (bf16[128,512]{1,0:T(8,128)(2,1)}, bf16[128,512]{1,0:T(8,128)(2,1)S(1)}, u32[]{:S(2)}, u32[]{:S(2)}) collective-permute-start(bf16[128,512]{1,0:T(8,128)(2,1)} %get-tuple-element.46.refs_4_.refs_6_), channel_id=1, source_target_pairs={{0,2},{1,3},{2,0},{3,1},{4,6},{5,7},{6,4},{7,5},{8,10},{9,11},{10,... | collective-permute-start | bytes 393224 | tf_op jit(solution)/shard_map/ppermute | solution.py:161
  25.7 13.1 %collective-permute-start.7 = (bf16[128,768]{1,0:T(8,128)(2,1)S(1)}, bf16[128,768]{1,0:T(8,128)(2,1)S(1)}, u32[]{:S(2)}, u32[]{:S(2)}) collective-permute-start(bf16[128,768]{1,0:T(8,128)(2,1)S(1)} %collective-permute-done.6.refs_0_.refs_4_), channel_id=1, source_target_pairs={{0,1},{1,0},{2,3},{3,2},{4,5},{5,4},{6,7},{7,6},{8,9},{9,8},{10,11... | collective-permute-start | bytes 589832 | tf_op jit(solution)/shard_map/ppermute | solution.py:161
  27.9 14.2 %collective-permute-start.4 = (bf16[128,2048]{1,0:T(8,128)(2,1)}, bf16[128,2048]{1,0:T(8,128)(2,1)S(1)}, u32[]{:S(2)}, u32[]{:S(2)}) collective-permute-start(bf16[128,2048]{1,0:T(8,128)(2,1)} %refs_3_.1), channel_id=1, source_target_pairs={{0,1},{1,0},{2,3},{3,2},{4,5},{5,4},{6,7},{7,6},{8,9},{9,8},{10,11... | collective-permute-start | bytes 1572872 | tf_op jit(solution)/shard_map/ppermute | solution.py:161
  30.7 8.2 %collective-permute-start.9 = (bf16[128,512]{1,0:T(8,128)(2,1)S(1)}, bf16[128,512]{1,0:T(8,128)(2,1)S(1)}, u32[]{:S(2)}, u32[]{:S(2)}) collective-permute-start(bf16[128,512]{1,0:T(8,128)(2,1)S(1)} %collective-permute-done.8.refs_2_.refs_8_), channel_id=1, source_target_pairs={{0,1},{1,0},{2,3},{3,2},{4,5},{5,4},{6,7},{7,6},{8,9},{9,8},{10,11... | collective-permute-start | bytes 393224 | tf_op jit(solution)/shard_map/ppermute | solution.py:161
  33.0 5.8 %collective-permute-start.11 = (bf16[128,512]{1,0:T(8,128)(2,1)S(1)}, bf16[128,512]{1,0:T(8,128)(2,1)S(1)}, u32[]{:S(2)}, u32[]{:S(2)}) collective-permute-start(bf16[128,512]{1,0:T(8,128)(2,1)S(1)} %collective-permute-done.10.refs_4_.refs_8_), channel_id=1, source_target_pairs={{0,1},{1,0},{2,3},{3,2},{4,5},{5,4},{6,7},{7,6},{8,9},{9,8},{10,11... | collective-permute-start | bytes 393224 | tf_op jit(solution)/shard_map/ppermute | solution.py:161
  33.0 1.0 %copy-start.3 = (bf16[128,2048]{1,0:T(8,128)(2,1)S(1)}, bf16[128,2048]{1,0:T(8,128)(2,1)}, u32[]{:S(2)}) copy-start(bf16[128,2048]{1,0:T(8,128)(2,1)} %refs_3_.1) | copy-start | bytes 1572868
  37.0 1.9 %collective-permute-start.13 = (bf16[128,384]{1,0:T(8,128)(2,1)S(1)}, bf16[128,384]{1,0:T(8,128)(2,1)S(1)}, u32[]{:S(2)}, u32[]{:S(2)}) collective-permute-start(bf16[128,384]{1,0:T(8,128)(2,1)S(1)} %collective-permute-done.12.refs_6_.refs_8_), channel_id=1, source_target_pairs={{0,1},{1,0},{2,3},{3,2},{4,5},{5,4},{6,7},{7,6},{8,9},{9,8},{10,11... | collective-permute-start | bytes 294920 | tf_op jit(solution)/shard_map/ppermute | solution.py:161
  38.9 2.1 %copy-start = (bf16[128,768]{1,0:T(8,128)(2,1)S(1)}, bf16[128,768]{1,0:T(8,128)(2,1)}, u32[]{:S(2)}) copy-start(bf16[128,768]{1,0:T(8,128)(2,1)} %get-tuple-element.44.refs_0_.refs_2_) | copy-start | bytes 589828
  38.9 2.6 %copy-start.2 = (bf16[128,512]{1,0:T(8,128)(2,1)S(1)}, bf16[128,512]{1,0:T(8,128)(2,1)}, u32[]{:S(2)}) copy-start(bf16[128,512]{1,0:T(8,128)(2,1)} %get-tuple-element.45.refs_2_.refs_6_) | copy-start | bytes 393220
  38.9 2.7 %copy-start.4 = (bf16[128,384]{1,0:T(8,128)(2,1)S(1)}, bf16[128,384]{1,0:T(8,128)(2,1)}, u32[]{:S(2)}) copy-start(bf16[128,384]{1,0:T(8,128)(2,1)} %get-tuple-element.47.refs_6_) | copy-start | bytes 294916
  38.9 3.1 %copy-start.1 = (bf16[128,512]{1,0:T(8,128)(2,1)S(1)}, bf16[128,512]{1,0:T(8,128)(2,1)}, u32[]{:S(2)}) copy-start(bf16[128,512]{1,0:T(8,128)(2,1)} %get-tuple-element.46.refs_4_.refs_6_) | copy-start | bytes 393220
  40.9 10.7 %collective-permute-start.16 = (bf16[128,2048]{1,0:T(8,128)(2,1)S(1)}, bf16[128,2048]{1,0:T(8,128)(2,1)S(1)}, u32[]{:S(2)}, u32[]{:S(2)}) collective-permute-start(bf16[128,2048]{1,0:T(8,128)(2,1)S(1)} %get-tuple-element.59), channel_id=1, source_target_pairs={{0,1},{1,0},{2,3},{3,2},{4,5},{5,4},{6,7},{7,6},{8,9},{9,8},{10,11... | collective-permute-start | bytes 1572872 | tf_op jit(solution)/shard_map/ppermute | solution.py:161
  41.0 2.5 %collective-permute-start = (bf16[128,768]{1,0:T(8,128)(2,1)S(1)}, bf16[128,768]{1,0:T(8,128)(2,1)S(1)}, u32[]{:S(2)}, u32[]{:S(2)}) collective-permute-start(bf16[128,768]{1,0:T(8,128)(2,1)S(1)} %copy-done), channel_id=1, source_target_pairs={{0,1},{1,0},{2,3},{3,2},{4,5},{5,4},{6,7},{7,6},{8,9},{9,8},{10,11... | collective-permute-start | bytes 589832 | tf_op jit(solution)/shard_map/ppermute | solution.py:161
  41.5 4.4 %collective-permute-start.1 = (bf16[128,512]{1,0:T(8,128)(2,1)S(1)}, bf16[128,512]{1,0:T(8,128)(2,1)S(1)}, u32[]{:S(2)}, u32[]{:S(2)}) collective-permute-start(bf16[128,512]{1,0:T(8,128)(2,1)S(1)} %copy-done.2), channel_id=1, source_target_pairs={{0,1},{1,0},{2,3},{3,2},{4,5},{5,4},{6,7},{7,6},{8,9},{9,8},{10,11... | collective-permute-start | bytes 393224 | tf_op jit(solution)/shard_map/ppermute | solution.py:161
  41.6 1.9 %collective-permute-start.3 = (bf16[128,384]{1,0:T(8,128)(2,1)S(1)}, bf16[128,384]{1,0:T(8,128)(2,1)S(1)}, u32[]{:S(2)}, u32[]{:S(2)}) collective-permute-start(bf16[128,384]{1,0:T(8,128)(2,1)S(1)} %copy-done.4), channel_id=1, source_target_pairs={{0,1},{1,0},{2,3},{3,2},{4,5},{5,4},{6,7},{7,6},{8,9},{9,8},{10,11... | collective-permute-start | bytes 294920 | tf_op jit(solution)/shard_map/ppermute | solution.py:161
  42.0 7.5 %collective-permute-start.2 = (bf16[128,512]{1,0:T(8,128)(2,1)S(1)}, bf16[128,512]{1,0:T(8,128)(2,1)S(1)}, u32[]{:S(2)}, u32[]{:S(2)}) collective-permute-start(bf16[128,512]{1,0:T(8,128)(2,1)S(1)} %copy-done.1), channel_id=1, source_target_pairs={{0,1},{1,0},{2,3},{3,2},{4,5},{5,4},{6,7},{7,6},{8,9},{9,8},{10,11... | collective-permute-start | bytes 393224 | tf_op jit(solution)/shard_map/ppermute | solution.py:161
  44.1 9.8 %collective-permute-start.27 = (bf16[4,64,384]{2,1,0:T(8,128)(2,1)S(1)}, bf16[4,64,384]{2,1,0:T(8,128)(2,1)S(1)}, u32[]{:S(2)}, u32[]{:S(2)}) collective-permute-start(bf16[4,64,384]{2,1,0:T(8,128)(2,1)S(1)} %get-tuple-element.81), channel_id=1, source_target_pairs={{0,4},{4,0},{8,12},{12,8},{16,20},{20,16},{24,28},{28,24},{1,5},{5... | collective-permute-start | bytes 589832 | tf_op jit(solution)/shard_map/ppermute | solution.py:161
  46.5 14.4 %collective-permute-start.21 = (bf16[4,64,512]{2,1,0:T(8,128)(2,1)S(1)}, bf16[4,64,512]{2,1,0:T(8,128)(2,1)S(1)}, u32[]{:S(2)}, u32[]{:S(2)}) collective-permute-start(bf16[4,64,512]{2,1,0:T(8,128)(2,1)S(1)} %get-tuple-element.69), channel_id=1, source_target_pairs={{0,8},{4,12},{8,0},{12,4},{16,24},{20,28},{24,16},{28,20},{1,9},{5... | collective-permute-start | bytes 786440 | tf_op jit(solution)/shard_map/ppermute | solution.py:161
  48.9 10.6 %collective-permute-start.18 = (bf16[4,64,640]{2,1,0:T(8,128)(2,1)S(1)}, bf16[4,64,640]{2,1,0:T(8,128)(2,1)S(1)}, u32[]{:S(2)}, u32[]{:S(2)}) collective-permute-start(bf16[4,64,640]{2,1,0:T(8,128)(2,1)S(1)} %get-tuple-element.63), channel_id=1, source_target_pairs={{0,4},{4,0},{8,12},{12,8},{16,20},{20,16},{24,28},{28,24},{1,5},{5... | collective-permute-start | bytes 983048 | tf_op jit(solution)/shard_map/ppermute | solution.py:161
  51.5 31.5 %collective-permute-start.5 = (bf16[128,2048]{1,0:T(8,128)(2,1)S(1)}, bf16[128,2048]{1,0:T(8,128)(2,1)S(1)}, u32[]{:S(2)}, u32[]{:S(2)}) collective-permute-start(bf16[128,2048]{1,0:T(8,128)(2,1)S(1)} %get-tuple-element.55), channel_id=1, source_target_pairs={{0,1},{1,0},{2,3},{3,2},{4,5},{5,4},{6,7},{7,6},{8,9},{9,8},{10,11... | collective-permute-start | bytes 1572872 | tf_op jit(solution)/shard_map/ppermute | solution.py:161
  51.7 31.3 %collective-permute-start.17 = (bf16[128,2048]{1,0:T(8,128)(2,1)S(1)}, bf16[128,2048]{1,0:T(8,128)(2,1)S(1)}, u32[]{:S(2)}, u32[]{:S(2)}) collective-permute-start(bf16[128,2048]{1,0:T(8,128)(2,1)S(1)} %shard_map.92), channel_id=1, source_target_pairs={{0,2},{1,3},{2,0},{3,1},{4,6},{5,7},{6,4},{7,5},{8,10},{9,11},{10,... | collective-permute-start | bytes 1572872 | tf_op jit(solution)/shard_map/ppermute | solution.py:161
  53.9 10.1 %collective-permute-start.24 = (bf16[4,64,512]{2,1,0:T(8,128)(2,1)S(1)}, bf16[4,64,512]{2,1,0:T(8,128)(2,1)S(1)}, u32[]{:S(2)}, u32[]{:S(2)}) collective-permute-start(bf16[4,64,512]{2,1,0:T(8,128)(2,1)S(1)} %get-tuple-element.75), channel_id=1, source_target_pairs={{0,4},{4,0},{8,12},{12,8},{16,20},{20,16},{24,28},{28,24},{1,5},{5... | collective-permute-start | bytes 786440 | tf_op jit(solution)/shard_map/ppermute | solution.py:161
  59.6 6.2 %collective-permute-start.28 = (bf16[2,64,384]{2,1,0:T(8,128)(2,1)S(1)}, bf16[2,64,384]{2,1,0:T(8,128)(2,1)S(1)}, u32[]{:S(2)}, u32[]{:S(2)}) collective-permute-start(bf16[2,64,384]{2,1,0:T(8,128)(2,1)S(1)} %get-tuple-element.83), channel_id=1, source_target_pairs={{0,8},{4,12},{8,0},{12,4},{16,24},{20,28},{24,16},{28,20},{1,9},{5... | collective-permute-start | bytes 294920 | tf_op jit(solution)/shard_map/ppermute | solution.py:161
  60.9 6.6 %collective-permute-start.19 = (bf16[2,64,640]{2,1,0:T(8,128)(2,1)S(1)}, bf16[2,64,640]{2,1,0:T(8,128)(2,1)S(1)}, u32[]{:S(2)}, u32[]{:S(2)}) collective-permute-start(bf16[2,64,640]{2,1,0:T(8,128)(2,1)S(1)} %get-tuple-element.65), channel_id=1, source_target_pairs={{0,8},{4,12},{8,0},{12,4},{16,24},{20,28},{24,16},{28,20},{1,9},{5... | collective-permute-start | bytes 491528 | tf_op jit(solution)/shard_map/ppermute | solution.py:161
  64.0 6.2 %collective-permute-start.22 = (bf16[2,64,512]{2,1,0:T(8,128)(2,1)S(1)}, bf16[2,64,512]{2,1,0:T(8,128)(2,1)S(1)}, u32[]{:S(2)}, u32[]{:S(2)}) collective-permute-start(bf16[2,64,512]{2,1,0:T(8,128)(2,1)S(1)} %get-tuple-element.71), channel_id=1, source_target_pairs={{0,4},{4,0},{8,12},{12,8},{16,20},{20,16},{24,28},{28,24},{1,5},{5... | collective-permute-start | bytes 393224 | tf_op jit(solution)/shard_map/ppermute | solution.py:161
  65.8 6.0 %collective-permute-start.25 = (bf16[2,64,512]{2,1,0:T(8,128)(2,1)S(1)}, bf16[2,64,512]{2,1,0:T(8,128)(2,1)S(1)}, u32[]{:S(2)}, u32[]{:S(2)}) collective-permute-start(bf16[2,64,512]{2,1,0:T(8,128)(2,1)S(1)} %get-tuple-element.77), channel_id=1, source_target_pairs={{0,8},{4,12},{8,0},{12,4},{16,24},{20,28},{24,16},{28,20},{1,9},{5... | collective-permute-start | bytes 393224 | tf_op jit(solution)/shard_map/ppermute | solution.py:161
  67.5 6.9 %collective-permute-start.29 = (bf16[1,64,384]{2,1,0:T(8,128)(2,1)S(1)}, bf16[1,64,384]{2,1,0:T(8,128)(2,1)S(1)}, u32[]{:S(2)}, u32[]{:S(2)}) collective-permute-start(bf16[1,64,384]{2,1,0:T(8,128)(2,1)S(1)} %get-tuple-element.85), channel_id=1, source_target_pairs={{0,16},{4,20},{8,24},{12,28},{16,0},{20,4},{24,8},{28,12},{1,17},{... | collective-permute-start | bytes 147464 | tf_op jit(solution)/shard_map/ppermute | solution.py:161
  70.2 12.0 %collective-permute-start.20 = (bf16[1,64,640]{2,1,0:T(8,128)(2,1)S(1)}, bf16[1,64,640]{2,1,0:T(8,128)(2,1)S(1)}, u32[]{:S(2)}, u32[]{:S(2)}) collective-permute-start(bf16[1,64,640]{2,1,0:T(8,128)(2,1)S(1)} %get-tuple-element.67), channel_id=1, source_target_pairs={{0,16},{4,20},{8,24},{12,28},{16,0},{20,4},{24,8},{28,12},{1,17},{... | collective-permute-start | bytes 245768 | tf_op jit(solution)/shard_map/ppermute | solution.py:161
  71.8 8.9 %collective-permute-start.23 = (bf16[1,64,512]{2,1,0:T(8,128)(2,1)S(1)}, bf16[1,64,512]{2,1,0:T(8,128)(2,1)S(1)}, u32[]{:S(2)}, u32[]{:S(2)}) collective-permute-start(bf16[1,64,512]{2,1,0:T(8,128)(2,1)S(1)} %get-tuple-element.73), channel_id=1, source_target_pairs={{0,16},{4,20},{8,24},{12,28},{16,0},{20,4},{24,8},{28,12},{1,17},{... | collective-permute-start | bytes 196616 | tf_op jit(solution)/shard_map/ppermute | solution.py:161
  74.4 7.8 %collective-permute-start.26 = (bf16[1,64,512]{2,1,0:T(8,128)(2,1)S(1)}, bf16[1,64,512]{2,1,0:T(8,128)(2,1)S(1)}, u32[]{:S(2)}, u32[]{:S(2)}) collective-permute-start(bf16[1,64,512]{2,1,0:T(8,128)(2,1)S(1)} %get-tuple-element.79), channel_id=1, source_target_pairs={{0,16},{4,20},{8,24},{12,28},{16,0},{20,4},{24,8},{28,12},{1,17},{... | collective-permute-start | bytes 196616 | tf_op jit(solution)/shard_map/ppermute | solution.py:161
where the time goes:
time: 84.2 us; the launch traced here: 84 us
  waiting for transfers between devices  36.4 us (43%)
  starting transfers between devices  29.4 us (35%)
  Pallas kernels  16.2 us (19%)
  local copies, waits for them, and re-layouts  1.06 us (1%)
  between operations  0.95 us (1%)
    ppermute x30, waiting for transfers between devices, swap(): return lax.ppermute(value, axis, [(i, i ^ 1 << bit) for i in range(size)])  36.4 us
    ppermute x30, starting transfers between devices, swap(): return lax.ppermute(value, axis, [(i, i ^ 1 << bit) for i in range(size)])  29.4 us
    pallas_call x21, Pallas kernels, call(): pl.pallas_call(kernel, out_shape=out_shapes, in_specs=[HBM_SPEC if in_hbm...  16.2 us
  transfers between devices with their start and end apart: 30, of which 10 were waited for; matrix products, arithmetic and copies ran while one was open for 0% of the time, Pallas kernels for 18%

commit v1 on v0

--- a/solution.py
+++ b/solution.py
@@ -12,7 +12,7 @@
 BF16 = jnp.bfloat16
 LANES = 128
 CHUNK_PARTS = (5, 4, 4, 3)
-FIRST_BIT = (0, 1, 0, 0)
+CHUNK_ORDERS = ((0, 1, 2), (1, 0, 2), (0, 1, 2), (0, 1, 2))
 CONTRACT_COLS = (((1,), (1,)), ((), ()))
 CONTRACT_ROWS = (((0,), (0,)), ((), ()))
 VMEM_SPEC = pl.BlockSpec(memory_space=pltpu.VMEM)
@@ -261,9 +261,7 @@
     block = hidden_width // dp
     down_terms = []
     for c in range(chunks):
-        order = list(range(dp_bits))
-        first = FIRST_BIT[c] if dp_bits > 1 else 0
-        order[0], order[first] = order[first], order[0]
+        order = CHUNK_ORDERS[c] if dp_bits == len(CHUNK_ORDERS[c]) else tuple(range(dp_bits))
         tagged = near_pieces[0] + far_pieces[0]
         parts = near_pieces[c] + far_pieces[c] if c else []
         send, keep = call(

time: 84.2 us -> 84.2 us (level)
  no operation moved by 1% of the time
where the time goes in v1:
time: 84.2 us; the launch traced here: 84 us
  waiting for transfers between devices  36.4 us (43%)
  starting transfers between devices  29.4 us (35%)
  Pallas kernels  16.2 us (19%)
  local copies, waits for them, and re-layouts  1.06 us (1%)
  between operations  0.95 us (1%)
    ppermute x30, waiting for transfers between devices, swap(): return lax.ppermute(value, axis, [(i, i ^ 1 << bit) for i in range(size)])  36.4 us
    ppermute x30, starting transfers between devices, swap(): return lax.ppermute(value, axis, [(i, i ^ 1 << bit) for i in range(size)])  29.4 us
    pallas_call x21, Pallas kernels, call(): pl.pallas_call(kernel, out_shape=out_shapes, in_specs=[HBM_SPEC if in_hbm...  16.2 us
  transfers between devices with their start and end apart: 30, of which 10 were waited for; matrix products, arithmetic and copies ran while one was open for 0% of the time, Pallas kernels for 18%

profile of v1, /device:TPU:0, one launch (start us, length us, event | category | flops | bytes accessed | tf_op | source)
XLA Modules:
  0.0 84.0 jit_solution(13679391164980069700)
XLA Ops:
  0.6 3.0 %collective-permute-start.14 = (bf16[128,2048]{1,0:T(8,128)(2,1)}, bf16[128,2048]{1,0:T(8,128)(2,1)S(1)}, u32[]{:S(2)}, u32[]{:S(2)}) collective-permute-start(bf16[128,2048]{1,0:T(8,128)(2,1)} %refs_3_.1), channel_id=1, source_target_pairs={{0,2},{1,3},{2,0},{3,1},{4,6},{5,7},{6,4},{7,5},{8,10},{9,11},{10,... | collective-permute-start | bytes 1572872 | tf_op jit(solution)/shard_map/ppermute | solution.py:161
  3.7 12.1 %collective-permute-done.14.refs_0_ = bf16[128,2048]{1,0:T(8,128)(2,1)S(1)} collective-permute-done((bf16[128,2048]{1,0:T(8,128)(2,1)}, bf16[128,2048]{1,0:T(8,128)(2,1)S(1)}, u32[]{:S(2)}, u32[]{:S(2)}) %collective-permute-start.14) | collective-permute-done | bytes 524320 | tf_op jit(solution)/shard_map/ppermute | solution.py:161
  15.8 1.9 %shard_map.86 = (bf16[128,768]{1,0:T(8,128)(2,1)}, bf16[128,512]{1,0:T(8,128)(2,1)}, bf16[128,512]{1,0:T(8,128)(2,1)}, bf16[128,384]{1,0:T(8,128)(2,1)}) custom-call(bf16[128,2048]{1,0:T(8,128)(2,1)} %refs_0_.1, s32[2,128]{1,0:T(2,128)} %bitcast.10, bf16[2,128]{1,0:T(2,128)(2,1)} %bitcast.11), custom_call_target="tpu_custom_call" | custom-call | bytes 1082880 | tf_op jit(solution)/shard_map/pallas_call | solution.py:25
  17.7 1.8 %collective-permute-start.6 = (bf16[128,768]{1,0:T(8,128)(2,1)}, bf16[128,768]{1,0:T(8,128)(2,1)S(1)}, u32[]{:S(2)}, u32[]{:S(2)}) collective-permute-start(bf16[128,768]{1,0:T(8,128)(2,1)} %get-tuple-element.44.refs_0_.refs_2_), channel_id=1, source_target_pairs={{0,2},{1,3},{2,0},{3,1},{4,6},{5,7},{6,4},{7,5},{8,10},{9,11},{10,... | collective-permute-start | bytes 589832 | tf_op jit(solution)/shard_map/ppermute | solution.py:161
  19.5 0.3 collective-permute-start.12
  19.8 1.7 %collective-permute-start.8 = (bf16[128,512]{1,0:T(8,128)(2,1)}, bf16[128,512]{1,0:T(8,128)(2,1)S(1)}, u32[]{:S(2)}, u32[]{:S(2)}) collective-permute-start(bf16[128,512]{1,0:T(8,128)(2,1)} %get-tuple-element.45.refs_2_.refs_6_), channel_id=1, source_target_pairs={{0,2},{1,3},{2,0},{3,1},{4,6},{5,7},{6,4},{7,5},{8,10},{9,11},{10,... | collective-permute-start | bytes 393224 | tf_op jit(solution)/shard_map/ppermute | solution.py:161
  21.5 0.3 collective-permute-start.10
  21.8 3.9 %collective-permute-done.6.refs_0_.refs_4_ = bf16[128,768]{1,0:T(8,128)(2,1)S(1)} collective-permute-done((bf16[128,768]{1,0:T(8,128)(2,1)}, bf16[128,768]{1,0:T(8,128)(2,1)S(1)}, u32[]{:S(2)}, u32[]{:S(2)}) %collective-permute-start.6) | collective-permute-done | bytes 196640 | tf_op jit(solution)/shard_map/ppermute | solution.py:161
  25.7 0.0 collective-permute-start.7
  25.7 2.1 %collective-permute-done.12.refs_6_.refs_8_ = bf16[128,384]{1,0:T(8,128)(2,1)S(1)} collective-permute-done((bf16[128,384]{1,0:T(8,128)(2,1)}, bf16[128,384]{1,0:T(8,128)(2,1)S(1)}, u32[]{:S(2)}, u32[]{:S(2)}) %collective-permute-start.12) | collective-permute-done | bytes 98336 | tf_op jit(solution)/shard_map/ppermute | solution.py:161
  27.9 0.0 collective-permute-start.4
  27.9 2.8 %collective-permute-done.8.refs_2_.refs_8_ = bf16[128,512]{1,0:T(8,128)(2,1)S(1)} collective-permute-done((bf16[128,512]{1,0:T(8,128)(2,1)}, bf16[128,512]{1,0:T(8,128)(2,1)S(1)}, u32[]{:S(2)}, u32[]{:S(2)}) %collective-permute-start.8) | collective-permute-done | bytes 131104 | tf_op jit(solution)/shard_map/ppermute | solution.py:161
  30.7 2.3 %collective-permute-done.10.refs_4_.refs_8_ = bf16[128,512]{1,0:T(8,128)(2,1)S(1)} collective-permute-done((bf16[128,512]{1,0:T(8,128)(2,1)}, bf16[128,512]{1,0:T(8,128)(2,1)S(1)}, u32[]{:S(2)}, u32[]{:S(2)}) %collective-permute-start.10) | collective-permute-done | bytes 131104 | tf_op jit(solution)/shard_map/ppermute | solution.py:161
  33.0 0.0 collective-permute-start.11
  33.0 1.0 %copy-done.3 = bf16[128,2048]{1,0:T(8,128)(2,1)S(1)} copy-done((bf16[128,2048]{1,0:T(8,128)(2,1)S(1)}, bf16[128,2048]{1,0:T(8,128)(2,1)}, u32[]{:S(2)}) %copy-start.3) | copy-done | bytes 524312
  34.1 2.9 %shard_map.87 = (bf16[2048,512]{1,0:T(8,128)(2,1)S(1)}, bf16[2048,512]{1,0:T(8,128)(2,1)S(1)}, bf16[512,2048]{1,0:T(8,128)(2,1)S(1)}, bf16[128,2048]{1,0:T(8,128)(2,1)S(1)}) custom-call(bf16[2048,512]{1,0:T(8,128)(2,1)} %bitcast.6, bf16[2048,512]{1,0:T(8,128)(2,1)} %bitcast.7, bf16[512,2048]{1,0:T(8,128)(2,1)} %bitcast.8, bf16[128,2048]{1,0:T(8,128)(2,1)S(1)} %copy-done.3), custom_call_target="tpu_custom_call" | custom-call | bytes 13631488 | tf_op jit(solution)/shard_map/pallas_call | solution.py:25
  37.0 0.0 collective-permute-done.15.refs_1_
  37.0 0.6 collective-permute-start.13
  37.5 1.3 %shard_map.90 = (bf16[256,512]{1,0:T(8,128)(2,1)S(1)}, f32[256,512]{1,0:T(8,128)S(1)}, f32[256,512]{1,0:T(8,128)S(1)}) custom-call(bf16[128,2048]{1,0:T(8,128)(2,1)S(1)} %collective-permute-done.14.refs_0_, bf16[128,2048]{1,0:T(8,128)(2,1)S(1)} %collective-permute-done.15.refs_1_, bf16[2048,512]{1,0:T(8,128)(2,1)S(1)} %get-tuple-element.49.refs_2_.refs_10_, ...), custom_call_target="tpu_custom_call" | custom-call | flops 1073741824 | bytes 6553600 | tf_op jit(solution)/shard_map/pallas_call | solution.py:25
  38.9 0.0 collective-permute-done.11.refs_5_.refs_9_
  38.9 0.0 collective-permute-done.7.refs_1_.refs_5_
  38.9 0.0 copy-start
  38.9 0.0 copy-start.2
  38.9 2.0 %shard_map.91 = (bf16[128,2048]{1,0:T(8,128)(2,1)S(1)}, bf16[128,2048]{1,0:T(8,128)(2,1)S(1)}) custom-call(bf16[128,768]{1,0:T(8,128)(2,1)S(1)} %collective-permute-done.6.refs_0_.refs_4_, bf16[128,768]{1,0:T(8,128)(2,1)S(1)} %collective-permute-done.7.refs_1_.refs_5_, bf16[128,512]{1,0:T(8,128)(2,1)S(1)} %collective-permute-done.8.refs_2_.refs_8_, ...), custom_call_target="tpu_custom_call" | custom-call | flops 1610612736 | bytes 9502720 | tf_op jit(solution)/shard_map/pallas_call | solution.py:25
  40.9 0.1 collective-permute-start.16
  41.0 0.5 collective-permute-start
  41.5 0.1 collective-permute-start.1
  41.6 0.4 collective-permute-start.3
  42.0 0.0 collective-permute-done.4.refs_1_
  42.0 0.1 collective-permute-start.2
  42.1 1.3 %shard_map.88 = (bf16[256,512]{1,0:T(8,128)(2,1)S(1)}, f32[256,512]{1,0:T(8,128)S(1)}, f32[256,512]{1,0:T(8,128)S(1)}) custom-call(bf16[128,2048]{1,0:T(8,128)(2,1)S(1)} %get-tuple-element.48.refs_0_, bf16[128,2048]{1,0:T(8,128)(2,1)S(1)} %collective-permute-done.4.refs_1_, bf16[2048,512]{1,0:T(8,128)(2,1)S(1)} %get-tuple-element.49.refs_2_.refs_10_, ...), custom_call_target="tpu_custom_call" | custom-call | flops 1073741824 | bytes 6553600 | tf_op jit(solution)/shard_map/pallas_call | solution.py:25
  43.4 0.1 collective-permute-done.3.refs_7_
  43.5 0.0 collective-permute-done.refs_1_.refs_3_
  43.5 0.6 shard_map.103
  44.1 1.8 %collective-permute-start.27 = (bf16[4,64,384]{2,1,0:T(8,128)(2,1)S(1)}, bf16[4,64,384]{2,1,0:T(8,128)(2,1)S(1)}, u32[]{:S(2)}, u32[]{:S(2)}) collective-permute-start(bf16[4,64,384]{2,1,0:T(8,128)(2,1)S(1)} %get-tuple-element.81), channel_id=1, source_target_pairs={{0,4},{4,0},{8,12},{12,8},{16,20},{20,16},{24,28},{28,24},{1,5},{5... | collective-permute-start | bytes 589832 | tf_op jit(solution)/shard_map/ppermute | solution.py:161
  45.9 0.6 shard_map.97
  46.5 1.7 %collective-permute-start.21 = (bf16[4,64,512]{2,1,0:T(8,128)(2,1)S(1)}, bf16[4,64,512]{2,1,0:T(8,128)(2,1)S(1)}, u32[]{:S(2)}, u32[]{:S(2)}) collective-permute-start(bf16[4,64,512]{2,1,0:T(8,128)(2,1)S(1)} %get-tuple-element.69), channel_id=1, source_target_pairs={{0,8},{4,12},{8,0},{12,4},{16,24},{20,28},{24,16},{28,20},{1,9},{5... | collective-permute-start | bytes 786440 | tf_op jit(solution)/shard_map/ppermute | solution.py:161
  48.2 0.8 shard_map.94
  48.9 0.6 collective-permute-start.18
  49.5 2.0 %shard_map.89 = (bf16[128,2048]{1,0:T(8,128)(2,1)S(1)}, bf16[128,2048]{1,0:T(8,128)(2,1)S(1)}) custom-call(bf16[128,768]{1,0:T(8,128)(2,1)S(1)} %copy-done, bf16[128,768]{1,0:T(8,128)(2,1)S(1)} %collective-permute-done.refs_1_.refs_3_, bf16[128,512]{1,0:T(8,128)(2,1)S(1)} %copy-done.2, bf16[128,512]{1,0:T(8,128)(2,1)S(1)} %collective-permute-done.1.refs_3_.refs_7_, ...), custom_call_target="tpu_custom_call" | custom-call | flops 1610612736 | bytes 9502720 | tf_op jit(solution)/shard_map/pallas_call | solution.py:25
  51.5 0.1 collective-permute-start.5
  51.6 0.0 collective-permute-done.16.refs_1_
  51.6 0.1 shard_map.92
  51.7 1.6 %collective-permute-start.17 = (bf16[128,2048]{1,0:T(8,128)(2,1)S(1)}, bf16[128,2048]{1,0:T(8,128)(2,1)S(1)}, u32[]{:S(2)}, u32[]{:S(2)}) collective-permute-start(bf16[128,2048]{1,0:T(8,128)(2,1)S(1)} %shard_map.92), channel_id=1, source_target_pairs={{0,2},{1,3},{2,0},{3,1},{4,6},{5,7},{6,4},{7,5},{8,10},{9,11},{10,... | collective-permute-start | bytes 1572872 | tf_op jit(solution)/shard_map/ppermute | solution.py:161
  53.3 0.6 shard_map.100
  53.9 1.6 %collective-permute-start.24 = (bf16[4,64,512]{2,1,0:T(8,128)(2,1)S(1)}, bf16[4,64,512]{2,1,0:T(8,128)(2,1)S(1)}, u32[]{:S(2)}, u32[]{:S(2)}) collective-permute-start(bf16[4,64,512]{2,1,0:T(8,128)(2,1)S(1)} %get-tuple-element.75), channel_id=1, source_target_pairs={{0,4},{4,0},{8,12},{12,8},{16,20},{20,16},{24,28},{28,24},{1,5},{5... | collective-permute-start | bytes 786440 | tf_op jit(solution)/shard_map/ppermute | solution.py:161
  55.5 0.1 shard_map.104
  55.6 4.0 %collective-permute-done.18.arrived = bf16[4,64,640]{2,1,0:T(8,128)(2,1)S(1)} collective-permute-done((bf16[4,64,640]{2,1,0:T(8,128)(2,1)S(1)}, bf16[4,64,640]{2,1,0:T(8,128)(2,1)S(1)}, u32[]{:S(2)}, u32[]{:S(2)}) %collective-permute-start.18) | collective-permute-done | bytes 327712 | tf_op jit(solution)/shard_map/ppermute | solution.py:161
  59.6 1.2 %collective-permute-start.28 = (bf16[2,64,384]{2,1,0:T(8,128)(2,1)S(1)}, bf16[2,64,384]{2,1,0:T(8,128)(2,1)S(1)}, u32[]{:S(2)}, u32[]{:S(2)}) collective-permute-start(bf16[2,64,384]{2,1,0:T(8,128)(2,1)S(1)} %get-tuple-element.83), channel_id=1, source_target_pairs={{0,8},{4,12},{8,0},{12,4},{16,24},{20,28},{24,16},{28,20},{1,9},{5... | collective-permute-start | bytes 294920 | tf_op jit(solution)/shard_map/ppermute | solution.py:161
  60.7 0.1 shard_map.95
  60.9 0.9 %collective-permute-start.19 = (bf16[2,64,640]{2,1,0:T(8,128)(2,1)S(1)}, bf16[2,64,640]{2,1,0:T(8,128)(2,1)S(1)}, u32[]{:S(2)}, u32[]{:S(2)}) collective-permute-start(bf16[2,64,640]{2,1,0:T(8,128)(2,1)S(1)} %get-tuple-element.65), channel_id=1, source_target_pairs={{0,8},{4,12},{8,0},{12,4},{16,24},{20,28},{24,16},{28,20},{1,9},{5... | collective-permute-start | bytes 491528 | tf_op jit(solution)/shard_map/ppermute | solution.py:161
  61.8 0.1 shard_map.98
  61.9 2.1 %collective-permute-done.24.arrived = bf16[4,64,512]{2,1,0:T(8,128)(2,1)S(1)} collective-permute-done((bf16[4,64,512]{2,1,0:T(8,128)(2,1)S(1)}, bf16[4,64,512]{2,1,0:T(8,128)(2,1)S(1)}, u32[]{:S(2)}, u32[]{:S(2)}) %collective-permute-start.24) | collective-permute-done | bytes 262176 | tf_op jit(solution)/shard_map/ppermute | solution.py:161
  64.0 1.7 %collective-permute-start.22 = (bf16[2,64,512]{2,1,0:T(8,128)(2,1)S(1)}, bf16[2,64,512]{2,1,0:T(8,128)(2,1)S(1)}, u32[]{:S(2)}, u32[]{:S(2)}) collective-permute-start(bf16[2,64,512]{2,1,0:T(8,128)(2,1)S(1)} %get-tuple-element.71), channel_id=1, source_target_pairs={{0,4},{4,0},{8,12},{12,8},{16,20},{20,16},{24,28},{28,24},{1,5},{5... | collective-permute-start | bytes 393224 | tf_op jit(solution)/shard_map/ppermute | solution.py:161
  65.7 0.1 shard_map.101
  65.8 1.6 %collective-permute-start.25 = (bf16[2,64,512]{2,1,0:T(8,128)(2,1)S(1)}, bf16[2,64,512]{2,1,0:T(8,128)(2,1)S(1)}, u32[]{:S(2)}, u32[]{:S(2)}) collective-permute-start(bf16[2,64,512]{2,1,0:T(8,128)(2,1)S(1)} %get-tuple-element.77), channel_id=1, source_target_pairs={{0,8},{4,12},{8,0},{12,4},{16,24},{20,28},{24,16},{28,20},{1,9},{5... | collective-permute-start | bytes 393224 | tf_op jit(solution)/shard_map/ppermute | solution.py:161
  67.5 2.7 %collective-permute-start.29 = (bf16[1,64,384]{2,1,0:T(8,128)(2,1)S(1)}, bf16[1,64,384]{2,1,0:T(8,128)(2,1)S(1)}, u32[]{:S(2)}, u32[]{:S(2)}) collective-permute-start(bf16[1,64,384]{2,1,0:T(8,128)(2,1)S(1)} %get-tuple-element.85), channel_id=1, source_target_pairs={{0,16},{4,20},{8,24},{12,28},{16,0},{20,4},{24,8},{28,12},{1,17},{... | collective-permute-start | bytes 147464 | tf_op jit(solution)/shard_map/ppermute | solution.py:161
  70.2 1.5 %collective-permute-start.20 = (bf16[1,64,640]{2,1,0:T(8,128)(2,1)S(1)}, bf16[1,64,640]{2,1,0:T(8,128)(2,1)S(1)}, u32[]{:S(2)}, u32[]{:S(2)}) collective-permute-start(bf16[1,64,640]{2,1,0:T(8,128)(2,1)S(1)} %get-tuple-element.67), channel_id=1, source_target_pairs={{0,16},{4,20},{8,24},{12,28},{16,0},{20,4},{24,8},{28,12},{1,17},{... | collective-permute-start | bytes 245768 | tf_op jit(solution)/shard_map/ppermute | solution.py:161
  71.8 2.5 %collective-permute-start.23 = (bf16[1,64,512]{2,1,0:T(8,128)(2,1)S(1)}, bf16[1,64,512]{2,1,0:T(8,128)(2,1)S(1)}, u32[]{:S(2)}, u32[]{:S(2)}) collective-permute-start(bf16[1,64,512]{2,1,0:T(8,128)(2,1)S(1)} %get-tuple-element.73), channel_id=1, source_target_pairs={{0,16},{4,20},{8,24},{12,28},{16,0},{20,4},{24,8},{28,12},{1,17},{... | collective-permute-start | bytes 196616 | tf_op jit(solution)/shard_map/ppermute | solution.py:161
  74.4 1.0 %collective-permute-start.26 = (bf16[1,64,512]{2,1,0:T(8,128)(2,1)S(1)}, bf16[1,64,512]{2,1,0:T(8,128)(2,1)S(1)}, u32[]{:S(2)}, u32[]{:S(2)}) collective-permute-start(bf16[1,64,512]{2,1,0:T(8,128)(2,1)S(1)} %get-tuple-element.79), channel_id=1, source_target_pairs={{0,16},{4,20},{8,24},{12,28},{16,0},{20,4},{24,8},{28,12},{1,17},{... | collective-permute-start | bytes 196616 | tf_op jit(solution)/shard_map/ppermute | solution.py:161
  75.4 5.3 %collective-permute-done.23.refs_3_ = bf16[1,64,512]{2,1,0:T(8,128)(2,1)S(1)} collective-permute-done((bf16[1,64,512]{2,1,0:T(8,128)(2,1)S(1)}, bf16[1,64,512]{2,1,0:T(8,128)(2,1)S(1)}, u32[]{:S(2)}, u32[]{:S(2)}) %collective-permute-start.23) | collective-permute-done | bytes 65568 | tf_op jit(solution)/shard_map/ppermute | solution.py:161
  80.7 1.5 %collective-permute-done.26.refs_5_ = bf16[1,64,512]{2,1,0:T(8,128)(2,1)S(1)} collective-permute-done((bf16[1,64,512]{2,1,0:T(8,128)(2,1)S(1)}, bf16[1,64,512]{2,1,0:T(8,128)(2,1)S(1)}, u32[]{:S(2)}, u32[]{:S(2)}) %collective-permute-start.26) | collective-permute-done | bytes 65568 | tf_op jit(solution)/shard_map/ppermute | solution.py:161
  82.2 0.8 shard_map.106
  83.0 1.0 %shard_map.93 = bf16[128,2048]{1,0:T(8,128)(2,1)} custom-call(bf16[128,2048]{1,0:T(8,128)(2,1)S(1)} %get-tuple-element.54.refs_0_, bf16[128,2048]{1,0:T(8,128)(2,1)S(1)} %collective-permute-done.5.refs_1_, bf16[128,2048]{1,0:T(8,128)(2,1)S(1)} %collective-permute-done.17.refs_2_), custom_call_target="tpu_custom_call" | custom-call | bytes 2097152 | tf_op jit(solution)/shard_map/pallas_call | solution.py:25
  (27 shorter events, 0.2 us)
Async XLA Ops:
  0.6 15.2 %collective-permute-start.14 = (bf16[128,2048]{1,0:T(8,128)(2,1)}, bf16[128,2048]{1,0:T(8,128)(2,1)S(1)}, u32[]{:S(2)}, u32[]{:S(2)}) collective-permute-start(bf16[128,2048]{1,0:T(8,128)(2,1)} %refs_3_.1), channel_id=1, source_target_pairs={{0,2},{1,3},{2,0},{3,1},{4,6},{5,7},{6,4},{7,5},{8,10},{9,11},{10,... | collective-permute-start | bytes 1572872 | tf_op jit(solution)/shard_map/ppermute | solution.py:161
  15.8 21.2 %collective-permute-start.15 = (bf16[128,2048]{1,0:T(8,128)(2,1)S(1)}, bf16[128,2048]{1,0:T(8,128)(2,1)S(1)}, u32[]{:S(2)}, u32[]{:S(2)}) collective-permute-start(bf16[128,2048]{1,0:T(8,128)(2,1)S(1)} %collective-permute-done.14.refs_0_), channel_id=1, source_target_pairs={{0,1},{1,0},{2,3},{3,2},{4,5},{5,4},{6,7},{7,6},{8,9},{9,8},{10,11... | collective-permute-start | bytes 1572872 | tf_op jit(solution)/shard_map/ppermute | solution.py:161
  17.7 8.0 %collective-permute-start.6 = (bf16[128,768]{1,0:T(8,128)(2,1)}, bf16[128,768]{1,0:T(8,128)(2,1)S(1)}, u32[]{:S(2)}, u32[]{:S(2)}) collective-permute-start(bf16[128,768]{1,0:T(8,128)(2,1)} %get-tuple-element.44.refs_0_.refs_2_), channel_id=1, source_target_pairs={{0,2},{1,3},{2,0},{3,1},{4,6},{5,7},{6,4},{7,5},{8,10},{9,11},{10,... | collective-permute-start | bytes 589832 | tf_op jit(solution)/shard_map/ppermute | solution.py:161
  19.5 8.4 %collective-permute-start.12 = (bf16[128,384]{1,0:T(8,128)(2,1)}, bf16[128,384]{1,0:T(8,128)(2,1)S(1)}, u32[]{:S(2)}, u32[]{:S(2)}) collective-permute-start(bf16[128,384]{1,0:T(8,128)(2,1)} %get-tuple-element.47.refs_6_), channel_id=1, source_target_pairs={{0,2},{1,3},{2,0},{3,1},{4,6},{5,7},{6,4},{7,5},{8,10},{9,11},{10,... | collective-permute-start | bytes 294920 | tf_op jit(solution)/shard_map/ppermute | solution.py:161
  19.8 10.9 %collective-permute-start.8 = (bf16[128,512]{1,0:T(8,128)(2,1)}, bf16[128,512]{1,0:T(8,128)(2,1)S(1)}, u32[]{:S(2)}, u32[]{:S(2)}) collective-permute-start(bf16[128,512]{1,0:T(8,128)(2,1)} %get-tuple-element.45.refs_2_.refs_6_), channel_id=1, source_target_pairs={{0,2},{1,3},{2,0},{3,1},{4,6},{5,7},{6,4},{7,5},{8,10},{9,11},{10,... | collective-permute-start | bytes 393224 | tf_op jit(solution)/shard_map/ppermute | solution.py:161
  21.5 11.5 %collective-permute-start.10 = (bf16[128,512]{1,0:T(8,128)(2,1)}, bf16[128,512]{1,0:T(8,128)(2,1)S(1)}, u32[]{:S(2)}, u32[]{:S(2)}) collective-permute-start(bf16[128,512]{1,0:T(8,128)(2,1)} %get-tuple-element.46.refs_4_.refs_6_), channel_id=1, source_target_pairs={{0,2},{1,3},{2,0},{3,1},{4,6},{5,7},{6,4},{7,5},{8,10},{9,11},{10,... | collective-permute-start | bytes 393224 | tf_op jit(solution)/shard_map/ppermute | solution.py:161
  25.7 13.1 %collective-permute-start.7 = (bf16[128,768]{1,0:T(8,128)(2,1)S(1)}, bf16[128,768]{1,0:T(8,128)(2,1)S(1)}, u32[]{:S(2)}, u32[]{:S(2)}) collective-permute-start(bf16[128,768]{1,0:T(8,128)(2,1)S(1)} %collective-permute-done.6.refs_0_.refs_4_), channel_id=1, source_target_pairs={{0,1},{1,0},{2,3},{3,2},{4,5},{5,4},{6,7},{7,6},{8,9},{9,8},{10,11... | collective-permute-start | bytes 589832 | tf_op jit(solution)/shard_map/ppermute | solution.py:161
  27.9 14.2 %collective-permute-start.4 = (bf16[128,2048]{1,0:T(8,128)(2,1)}, bf16[128,2048]{1,0:T(8,128)(2,1)S(1)}, u32[]{:S(2)}, u32[]{:S(2)}) collective-permute-start(bf16[128,2048]{1,0:T(8,128)(2,1)} %refs_3_.1), channel_id=1, source_target_pairs={{0,1},{1,0},{2,3},{3,2},{4,5},{5,4},{6,7},{7,6},{8,9},{9,8},{10,11... | collective-permute-start | bytes 1572872 | tf_op jit(solution)/shard_map/ppermute | solution.py:161
  30.7 8.2 %collective-permute-start.9 = (bf16[128,512]{1,0:T(8,128)(2,1)S(1)}, bf16[128,512]{1,0:T(8,128)(2,1)S(1)}, u32[]{:S(2)}, u32[]{:S(2)}) collective-permute-start(bf16[128,512]{1,0:T(8,128)(2,1)S(1)} %collective-permute-done.8.refs_2_.refs_8_), channel_id=1, source_target_pairs={{0,1},{1,0},{2,3},{3,2},{4,5},{5,4},{6,7},{7,6},{8,9},{9,8},{10,11... | collective-permute-start | bytes 393224 | tf_op jit(solution)/shard_map/ppermute | solution.py:161
  33.0 5.8 %collective-permute-start.11 = (bf16[128,512]{1,0:T(8,128)(2,1)S(1)}, bf16[128,512]{1,0:T(8,128)(2,1)S(1)}, u32[]{:S(2)}, u32[]{:S(2)}) collective-permute-start(bf16[128,512]{1,0:T(8,128)(2,1)S(1)} %collective-permute-done.10.refs_4_.refs_8_), channel_id=1, source_target_pairs={{0,1},{1,0},{2,3},{3,2},{4,5},{5,4},{6,7},{7,6},{8,9},{9,8},{10,11... | collective-permute-start | bytes 393224 | tf_op jit(solution)/shard_map/ppermute | solution.py:161
  33.0 1.0 %copy-start.3 = (bf16[128,2048]{1,0:T(8,128)(2,1)S(1)}, bf16[128,2048]{1,0:T(8,128)(2,1)}, u32[]{:S(2)}) copy-start(bf16[128,2048]{1,0:T(8,128)(2,1)} %refs_3_.1) | copy-start | bytes 1572868
  37.0 1.9 %collective-permute-start.13 = (bf16[128,384]{1,0:T(8,128)(2,1)S(1)}, bf16[128,384]{1,0:T(8,128)(2,1)S(1)}, u32[]{:S(2)}, u32[]{:S(2)}) collective-permute-start(bf16[128,384]{1,0:T(8,128)(2,1)S(1)} %collective-permute-done.12.refs_6_.refs_8_), channel_id=1, source_target_pairs={{0,1},{1,0},{2,3},{3,2},{4,5},{5,4},{6,7},{7,6},{8,9},{9,8},{10,11... | collective-permute-start | bytes 294920 | tf_op jit(solution)/shard_map/ppermute | solution.py:161
  38.9 2.1 %copy-start = (bf16[128,768]{1,0:T(8,128)(2,1)S(1)}, bf16[128,768]{1,0:T(8,128)(2,1)}, u32[]{:S(2)}) copy-start(bf16[128,768]{1,0:T(8,128)(2,1)} %get-tuple-element.44.refs_0_.refs_2_) | copy-start | bytes 589828
  38.9 2.6 %copy-start.2 = (bf16[128,512]{1,0:T(8,128)(2,1)S(1)}, bf16[128,512]{1,0:T(8,128)(2,1)}, u32[]{:S(2)}) copy-start(bf16[128,512]{1,0:T(8,128)(2,1)} %get-tuple-element.45.refs_2_.refs_6_) | copy-start | bytes 393220
  38.9 2.7 %copy-start.4 = (bf16[128,384]{1,0:T(8,128)(2,1)S(1)}, bf16[128,384]{1,0:T(8,128)(2,1)}, u32[]{:S(2)}) copy-start(bf16[128,384]{1,0:T(8,128)(2,1)} %get-tuple-element.47.refs_6_) | copy-start | bytes 294916
  38.9 3.1 %copy-start.1 = (bf16[128,512]{1,0:T(8,128)(2,1)S(1)}, bf16[128,512]{1,0:T(8,128)(2,1)}, u32[]{:S(2)}) copy-start(bf16[128,512]{1,0:T(8,128)(2,1)} %get-tuple-element.46.refs_4_.refs_6_) | copy-start | bytes 393220
  40.9 10.7 %collective-permute-start.16 = (bf16[128,2048]{1,0:T(8,128)(2,1)S(1)}, bf16[128,2048]{1,0:T(8,128)(2,1)S(1)}, u32[]{:S(2)}, u32[]{:S(2)}) collective-permute-start(bf16[128,2048]{1,0:T(8,128)(2,1)S(1)} %get-tuple-element.59), channel_id=1, source_target_pairs={{0,1},{1,0},{2,3},{3,2},{4,5},{5,4},{6,7},{7,6},{8,9},{9,8},{10,11... | collective-permute-start | bytes 1572872 | tf_op jit(solution)/shard_map/ppermute | solution.py:161
  41.0 2.5 %collective-permute-start = (bf16[128,768]{1,0:T(8,128)(2,1)S(1)}, bf16[128,768]{1,0:T(8,128)(2,1)S(1)}, u32[]{:S(2)}, u32[]{:S(2)}) collective-permute-start(bf16[128,768]{1,0:T(8,128)(2,1)S(1)} %copy-done), channel_id=1, source_target_pairs={{0,1},{1,0},{2,3},{3,2},{4,5},{5,4},{6,7},{7,6},{8,9},{9,8},{10,11... | collective-permute-start | bytes 589832 | tf_op jit(solution)/shard_map/ppermute | solution.py:161
  41.5 4.4 %collective-permute-start.1 = (bf16[128,512]{1,0:T(8,128)(2,1)S(1)}, bf16[128,512]{1,0:T(8,128)(2,1)S(1)}, u32[]{:S(2)}, u32[]{:S(2)}) collective-permute-start(bf16[128,512]{1,0:T(8,128)(2,1)S(1)} %copy-done.2), channel_id=1, source_target_pairs={{0,1},{1,0},{2,3},{3,2},{4,5},{5,4},{6,7},{7,6},{8,9},{9,8},{10,11... | collective-permute-start | bytes 393224 | tf_op jit(solution)/shard_map/ppermute | solution.py:161
  41.6 1.9 %collective-permute-start.3 = (bf16[128,384]{1,0:T(8,128)(2,1)S(1)}, bf16[128,384]{1,0:T(8,128)(2,1)S(1)}, u32[]{:S(2)}, u32[]{:S(2)}) collective-permute-start(bf16[128,384]{1,0:T(8,128)(2,1)S(1)} %copy-done.4), channel_id=1, source_target_pairs={{0,1},{1,0},{2,3},{3,2},{4,5},{5,4},{6,7},{7,6},{8,9},{9,8},{10,11... | collective-permute-start | bytes 294920 | tf_op jit(solution)/shard_map/ppermute | solution.py:161
  42.0 7.5 %collective-permute-start.2 = (bf16[128,512]{1,0:T(8,128)(2,1)S(1)}, bf16[128,512]{1,0:T(8,128)(2,1)S(1)}, u32[]{:S(2)}, u32[]{:S(2)}) collective-permute-start(bf16[128,512]{1,0:T(8,128)(2,1)S(1)} %copy-done.1), channel_id=1, source_target_pairs={{0,1},{1,0},{2,3},{3,2},{4,5},{5,4},{6,7},{7,6},{8,9},{9,8},{10,11... | collective-permute-start | bytes 393224 | tf_op jit(solution)/shard_map/ppermute | solution.py:161
  44.1 9.8 %collective-permute-start.27 = (bf16[4,64,384]{2,1,0:T(8,128)(2,1)S(1)}, bf16[4,64,384]{2,1,0:T(8,128)(2,1)S(1)}, u32[]{:S(2)}, u32[]{:S(2)}) collective-permute-start(bf16[4,64,384]{2,1,0:T(8,128)(2,1)S(1)} %get-tuple-element.81), channel_id=1, source_target_pairs={{0,4},{4,0},{8,12},{12,8},{16,20},{20,16},{24,28},{28,24},{1,5},{5... | collective-permute-start | bytes 589832 | tf_op jit(solution)/shard_map/ppermute | solution.py:161
  46.5 14.4 %collective-permute-start.21 = (bf16[4,64,512]{2,1,0:T(8,128)(2,1)S(1)}, bf16[4,64,512]{2,1,0:T(8,128)(2,1)S(1)}, u32[]{:S(2)}, u32[]{:S(2)}) collective-permute-start(bf16[4,64,512]{2,1,0:T(8,128)(2,1)S(1)} %get-tuple-element.69), channel_id=1, source_target_pairs={{0,8},{4,12},{8,0},{12,4},{16,24},{20,28},{24,16},{28,20},{1,9},{5... | collective-permute-start | bytes 786440 | tf_op jit(solution)/shard_map/ppermute | solution.py:161
  48.9 10.6 %collective-permute-start.18 = (bf16[4,64,640]{2,1,0:T(8,128)(2,1)S(1)}, bf16[4,64,640]{2,1,0:T(8,128)(2,1)S(1)}, u32[]{:S(2)}, u32[]{:S(2)}) collective-permute-start(bf16[4,64,640]{2,1,0:T(8,128)(2,1)S(1)} %get-tuple-element.63), channel_id=1, source_target_pairs={{0,4},{4,0},{8,12},{12,8},{16,20},{20,16},{24,28},{28,24},{1,5},{5... | collective-permute-start | bytes 983048 | tf_op jit(solution)/shard_map/ppermute | solution.py:161
  51.5 31.5 %collective-permute-start.5 = (bf16[128,2048]{1,0:T(8,128)(2,1)S(1)}, bf16[128,2048]{1,0:T(8,128)(2,1)S(1)}, u32[]{:S(2)}, u32[]{:S(2)}) collective-permute-start(bf16[128,2048]{1,0:T(8,128)(2,1)S(1)} %get-tuple-element.55), channel_id=1, source_target_pairs={{0,1},{1,0},{2,3},{3,2},{4,5},{5,4},{6,7},{7,6},{8,9},{9,8},{10,11... | collective-permute-start | bytes 1572872 | tf_op jit(solution)/shard_map/ppermute | solution.py:161
  51.7 31.3 %collective-permute-start.17 = (bf16[128,2048]{1,0:T(8,128)(2,1)S(1)}, bf16[128,2048]{1,0:T(8,128)(2,1)S(1)}, u32[]{:S(2)}, u32[]{:S(2)}) collective-permute-start(bf16[128,2048]{1,0:T(8,128)(2,1)S(1)} %shard_map.92), channel_id=1, source_target_pairs={{0,2},{1,3},{2,0},{3,1},{4,6},{5,7},{6,4},{7,5},{8,10},{9,11},{10,... | collective-permute-start | bytes 1572872 | tf_op jit(solution)/shard_map/ppermute | solution.py:161
  53.9 10.1 %collective-permute-start.24 = (bf16[4,64,512]{2,1,0:T(8,128)(2,1)S(1)}, bf16[4,64,512]{2,1,0:T(8,128)(2,1)S(1)}, u32[]{:S(2)}, u32[]{:S(2)}) collective-permute-start(bf16[4,64,512]{2,1,0:T(8,128)(2,1)S(1)} %get-tuple-element.75), channel_id=1, source_target_pairs={{0,4},{4,0},{8,12},{12,8},{16,20},{20,16},{24,28},{28,24},{1,5},{5... | collective-permute-start | bytes 786440 | tf_op jit(solution)/shard_map/ppermute | solution.py:161
  59.6 6.2 %collective-permute-start.28 = (bf16[2,64,384]{2,1,0:T(8,128)(2,1)S(1)}, bf16[2,64,384]{2,1,0:T(8,128)(2,1)S(1)}, u32[]{:S(2)}, u32[]{:S(2)}) collective-permute-start(bf16[2,64,384]{2,1,0:T(8,128)(2,1)S(1)} %get-tuple-element.83), channel_id=1, source_target_pairs={{0,8},{4,12},{8,0},{12,4},{16,24},{20,28},{24,16},{28,20},{1,9},{5... | collective-permute-start | bytes 294920 | tf_op jit(solution)/shard_map/ppermute | solution.py:161
  60.9 6.6 %collective-permute-start.19 = (bf16[2,64,640]{2,1,0:T(8,128)(2,1)S(1)}, bf16[2,64,640]{2,1,0:T(8,128)(2,1)S(1)}, u32[]{:S(2)}, u32[]{:S(2)}) collective-permute-start(bf16[2,64,640]{2,1,0:T(8,128)(2,1)S(1)} %get-tuple-element.65), channel_id=1, source_target_pairs={{0,8},{4,12},{8,0},{12,4},{16,24},{20,28},{24,16},{28,20},{1,9},{5... | collective-permute-start | bytes 491528 | tf_op jit(solution)/shard_map/ppermute | solution.py:161
  64.0 6.2 %collective-permute-start.22 = (bf16[2,64,512]{2,1,0:T(8,128)(2,1)S(1)}, bf16[2,64,512]{2,1,0:T(8,128)(2,1)S(1)}, u32[]{:S(2)}, u32[]{:S(2)}) collective-permute-start(bf16[2,64,512]{2,1,0:T(8,128)(2,1)S(1)} %get-tuple-element.71), channel_id=1, source_target_pairs={{0,4},{4,0},{8,12},{12,8},{16,20},{20,16},{24,28},{28,24},{1,5},{5... | collective-permute-start | bytes 393224 | tf_op jit(solution)/shard_map/ppermute | solution.py:161
  65.8 6.0 %collective-permute-start.25 = (bf16[2,64,512]{2,1,0:T(8,128)(2,1)S(1)}, bf16[2,64,512]{2,1,0:T(8,128)(2,1)S(1)}, u32[]{:S(2)}, u32[]{:S(2)}) collective-permute-start(bf16[2,64,512]{2,1,0:T(8,128)(2,1)S(1)} %get-tuple-element.77), channel_id=1, source_target_pairs={{0,8},{4,12},{8,0},{12,4},{16,24},{20,28},{24,16},{28,20},{1,9},{5... | collective-permute-start | bytes 393224 | tf_op jit(solution)/shard_map/ppermute | solution.py:161
  67.5 6.9 %collective-permute-start.29 = (bf16[1,64,384]{2,1,0:T(8,128)(2,1)S(1)}, bf16[1,64,384]{2,1,0:T(8,128)(2,1)S(1)}, u32[]{:S(2)}, u32[]{:S(2)}) collective-permute-start(bf16[1,64,384]{2,1,0:T(8,128)(2,1)S(1)} %get-tuple-element.85), channel_id=1, source_target_pairs={{0,16},{4,20},{8,24},{12,28},{16,0},{20,4},{24,8},{28,12},{1,17},{... | collective-permute-start | bytes 147464 | tf_op jit(solution)/shard_map/ppermute | solution.py:161
  70.2 12.0 %collective-permute-start.20 = (bf16[1,64,640]{2,1,0:T(8,128)(2,1)S(1)}, bf16[1,64,640]{2,1,0:T(8,128)(2,1)S(1)}, u32[]{:S(2)}, u32[]{:S(2)}) collective-permute-start(bf16[1,64,640]{2,1,0:T(8,128)(2,1)S(1)} %get-tuple-element.67), channel_id=1, source_target_pairs={{0,16},{4,20},{8,24},{12,28},{16,0},{20,4},{24,8},{28,12},{1,17},{... | collective-permute-start | bytes 245768 | tf_op jit(solution)/shard_map/ppermute | solution.py:161
  71.8 8.9 %collective-permute-start.23 = (bf16[1,64,512]{2,1,0:T(8,128)(2,1)S(1)}, bf16[1,64,512]{2,1,0:T(8,128)(2,1)S(1)}, u32[]{:S(2)}, u32[]{:S(2)}) collective-permute-start(bf16[1,64,512]{2,1,0:T(8,128)(2,1)S(1)} %get-tuple-element.73), channel_id=1, source_target_pairs={{0,16},{4,20},{8,24},{12,28},{16,0},{20,4},{24,8},{28,12},{1,17},{... | collective-permute-start | bytes 196616 | tf_op jit(solution)/shard_map/ppermute | solution.py:161
  74.4 7.8 %collective-permute-start.26 = (bf16[1,64,512]{2,1,0:T(8,128)(2,1)S(1)}, bf16[1,64,512]{2,1,0:T(8,128)(2,1)S(1)}, u32[]{:S(2)}, u32[]{:S(2)}) collective-permute-start(bf16[1,64,512]{2,1,0:T(8,128)(2,1)S(1)} %get-tuple-element.79), channel_id=1, source_target_pairs={{0,16},{4,20},{8,24},{12,28},{16,0},{20,4},{24,8},{28,12},{1,17},{... | collective-permute-start | bytes 196616 | tf_op jit(solution)/shard_map/ppermute | solution.py:161
